TPU v7x, 32 devices: a whole 2x2x4 slice. The times are simulated.
32 devices in a mesh: tm: 16 (over z, y, x), tensor: 2 (over core).
Axes of the slice: x: 2, y: 2, z: 4, core: 2. Of those that a mesh axis runs over, the one named last changes fastest.
Arguments:
- noise_start: float32 [1, 16384], replicated, may hold values from -6 to 6
- timesteps: int32 [17], replicated, may hold values from 0 to 599, as said below
- class_labels: int32 [16, 1], P('tm'), may hold values from 0 to 999
- mixing: float32 [2, 16], P(None, 'tm'), may hold values from -0.5 to 0.5
- class_table: bfloat16 [1000, 768], replicated, may hold values from -3 to 3
- time_in: bfloat16 [256, 768], replicated, may hold values from -0.75 to 0.75
- time_out: bfloat16 [768, 768], replicated, may hold values from -0.21875 to 0.21875
- ada_weight: bfloat16 [768, 4608], replicated, may hold values from -0.21875 to 0.21875
- final_ada: bfloat16 [768, 1536], replicated, may hold values from -0.21875 to 0.21875
- patch_weight: bfloat16 [16, 768], replicated, may hold values from -1.5 to 1.5
- q_weight: bfloat16 [768, 768], replicated, may hold values from -1.5 to 1.5
- kv_weight: bfloat16 [768, 1536], replicated, may hold values from -1.5 to 1.5
- out_weight: bfloat16 [768, 768], replicated, may hold values from -0.4375 to 0.4375
- up_weight: bfloat16 [768, 3072], P(None, 'tensor'), may hold values from -0.21875 to 0.21875
- down_weight: bfloat16 [3072, 768], P('tensor'), may hold values from -0.21875 to 0.21875
- final_weight: bfloat16 [768, 16], replicated, may hold values from -0.21875 to 0.21875
Outputs:
- states: float32 [16, 1, 16384], P('tm')
- residuals: float32 [2, 16], P(None, 'tm')
Inputs may be any that keep to these rules, and one draw needn't show every extreme that they name: `timesteps`: strictly decreasing; the first is 599, the last is 0, all others lie from 100 to 549.
All inputs are finite; a program needn't handle non-finite values.
Results may differ from a plain program's by a relative error of at most 0.008.
Values may be sent and summed in bfloat16 or wider, within the bound.
A program may use at most 128 MiB of HBM per device.

v0:
```python
import math

import jax
import jax.numpy as jnp
from jax import lax
from jax.sharding import PartitionSpec as P

D = 768
HEADS = 12
SEQ = 1024
PATCH = 16
CLASSES = 1000
FREQ = 256
IMG = 1
ITERS = 2
LAT = 16384


norm_eps = 1e-06
plan_steps = 1000


def prefix(array, axis, combine, identity):
    size, here = (lax.axis_size(axis), lax.axis_index(axis))
    everything = lax.all_gather(
        array.astype(jnp.bfloat16 if array.dtype == jnp.float32 else array.dtype), axis
    )
    start = jnp.broadcast_to(jnp.asarray(identity, array.dtype), array.shape)

    def step(k, before):
        reached = k < here
        new = combine(before, everything[k].astype(array.dtype))
        return jnp.where(reached, new, before)

    return lax.fori_loop(0, size, step, start)


def shortened(array):
    return jax.tree.map(lambda a: a.astype(jnp.bfloat16) if a.dtype == jnp.float32 else a, array)


def from_behind(value, axis, steps):
    count = lax.axis_size(axis)
    leading, last = (max(0, -steps), min(count, count - steps))
    return lax.ppermute(value, axis, [(source, source + steps) for source in range(leading, last)])


def log_table():
    levels = jnp.arange(plan_steps, dtype=jnp.float32)
    beta_values = 0.0001 + (0.02 - 0.0001) * levels / (plan_steps - 1)
    return jnp.cumsum(jnp.log(1.0 - beta_values))


def alpha_at(moments):
    matches = moments[:, None] == jnp.arange(plan_steps, dtype=jnp.int32)[None, :]
    return jnp.exp(jnp.sum(jnp.where(matches, log_table()[None, :], 0.0), axis=1))


def time_features(moment):
    half_count = FREQ // 2
    freq_rates = jnp.exp(
        -math.log(10000.0) * jnp.arange(half_count, dtype=jnp.float32) / half_count
    )
    angles = moment.astype(jnp.float32) * freq_rates
    return jnp.concatenate([jnp.cos(angles), jnp.sin(angles)])[None, :]


def positions():
    half_width = D // 2
    places = jnp.arange(SEQ, dtype=jnp.float32)[:, None]
    freq_rates = jnp.exp(
        -math.log(10000.0) * jnp.arange(half_width, dtype=jnp.float32) / half_width
    )
    angles = places * freq_rates[None, :]
    return jnp.concatenate([jnp.sin(angles), jnp.cos(angles)], axis=1)


def layer_norm(values):
    center = values - jnp.mean(values, axis=-1, keepdims=True)
    spread = jnp.mean(center * center, axis=-1, keepdims=True)
    return center * lax.rsqrt(spread + norm_eps)


def modulate(values, shift, scale):
    return layer_norm(values) * (1.0 + scale) + shift


def split_rows(matrix, count):
    return [matrix[:, None, column * D : (column + 1) * D] for column in range(count)]


def add_fields(earlier, later_part):
    return earlier + later_part


def pick_entry(vector, wanted):
    matches = jnp.arange(vector.shape[0], dtype=jnp.int32) == wanted
    return jnp.sum(jnp.where(matches, vector, 0))


def per_device(
    noise_start,
    timesteps,
    class_labels,
    mixing,
    class_table,
    time_in,
    time_out,
    ada_weight,
    final_ada,
    patch_weight,
    q_weight,
    kv_weight,
    out_weight,
    up_weight,
    down_weight,
    final_weight,
):
    window_point = lax.axis_index("tm")
    group_size = lax.axis_size("tensor")
    member = lax.axis_index("tensor")
    rows_own = SEQ // group_size
    offset = member * rows_own
    head_dim = D // HEADS
    moment_now = pick_entry(timesteps, window_point)
    moment_next = pick_entry(timesteps, window_point + 1)
    alphas = alpha_at(jnp.stack([moment_now, moment_next]))
    keep_coef = jnp.sqrt(alphas[1] / alphas[0])
    noise_coef = jnp.sqrt(1.0 - alphas[1]) - jnp.sqrt(alphas[1] * (1.0 - alphas[0]) / alphas[0])
    features = time_features(moment_now).astype(jnp.bfloat16)
    time_hidden = jax.nn.silu(
        jnp.dot(features, time_in, preferred_element_type=jnp.float32)
    ).astype(jnp.bfloat16)
    time_embed = jnp.dot(time_hidden, time_out, preferred_element_type=jnp.float32)
    onehot = (class_labels[0][:, None] == jnp.arange(CLASSES, dtype=jnp.int32)[None, :]).astype(
        jnp.bfloat16
    )
    classes = jnp.dot(onehot, class_table, preferred_element_type=jnp.float32)
    summed = jax.nn.silu(time_embed + classes).astype(jnp.bfloat16)
    modul = jnp.dot(summed, ada_weight, preferred_element_type=jnp.float32)
    final_mod = jnp.dot(summed, final_ada, preferred_element_type=jnp.float32)
    shift_attn, scale_attn, gate_attn, shift_mlp, scale_mlp, gate_mlp = split_rows(modul, 6)
    shift_out, scale_out = split_rows(final_mod, 2)
    place_rows = lax.dynamic_slice_in_dim(positions(), offset, rows_own, 0)
    state_in = noise_start
    state_out = noise_start
    previous = noise_start
    residual_rows = []
    for iteration in range(ITERS):
        tokens = state_in.astype(jnp.bfloat16).reshape(IMG, SEQ, PATCH)
        own_tokens = lax.dynamic_slice_in_dim(tokens, offset, rows_own, 1).reshape(
            IMG * rows_own, PATCH
        )
        hidden = jnp.dot(own_tokens, patch_weight, preferred_element_type=jnp.float32).reshape(
            IMG, rows_own, D
        )
        hidden = hidden + place_rows[None]
        attn_in = (
            modulate(hidden, shift_attn, scale_attn).astype(jnp.bfloat16).reshape(IMG * rows_own, D)
        )
        queries = jnp.dot(attn_in, q_weight, preferred_element_type=jnp.float32).astype(
            jnp.bfloat16
        )
        queries = queries.reshape(IMG, rows_own, HEADS, head_dim)
        key_value = jnp.dot(attn_in, kv_weight, preferred_element_type=jnp.float32).astype(
            jnp.bfloat16
        )
        key_value = key_value.reshape(IMG, rows_own, 2 * D)
        gathered = lax.all_gather(key_value, "tensor", axis=1, tiled=True)
        key_heads = gathered[:, :, :D].reshape(IMG, SEQ, HEADS, head_dim)
        value_heads = gathered[:, :, D:].reshape(IMG, SEQ, HEADS, head_dim)
        scores = jnp.einsum(
            "bqhd,bkhd->bhqk", queries, key_heads, preferred_element_type=jnp.float32
        )
        scores = scores * (1.0 / math.sqrt(head_dim))
        attention = jax.nn.softmax(scores, axis=-1).astype(jnp.bfloat16)
        attended = jnp.einsum(
            "bhqk,bkhd->bqhd", attention, value_heads, preferred_element_type=jnp.float32
        )
        attended = attended.astype(jnp.bfloat16).reshape(IMG * rows_own, D)
        projected = jnp.dot(attended, out_weight, preferred_element_type=jnp.float32).reshape(
            IMG, rows_own, D
        )
        hidden = hidden + gate_attn * projected
        stream = lax.all_gather(hidden.astype(jnp.bfloat16), "tensor", axis=1, tiled=True).astype(
            hidden.dtype
        )
        predict_mlp_in = modulate(stream, shift_mlp, scale_mlp).astype(jnp.bfloat16)
        flat_in = predict_mlp_in.reshape(IMG * SEQ, D)
        lifted = jax.nn.gelu(
            jnp.dot(flat_in, up_weight, preferred_element_type=jnp.float32), approximate=True
        )
        lifted = lifted.astype(jnp.bfloat16)
        mlp_sum = lax.psum(
            jnp.dot(lifted, down_weight, preferred_element_type=jnp.float32)
            .reshape(IMG, SEQ, D)
            .astype(jnp.bfloat16),
            "tensor",
        ).astype(jnp.float32)
        stream_out = stream + gate_mlp * mlp_sum
        final_in = (
            modulate(stream_out, shift_out, scale_out).astype(jnp.bfloat16).reshape(IMG * SEQ, D)
        )
        predicted = jnp.dot(final_in, final_weight, preferred_element_type=jnp.float32).reshape(
            IMG, LAT
        )
        drift_now = (keep_coef - 1.0) * state_in + noise_coef * predicted
        slice_width = LAT // group_size
        drift_piece = lax.dynamic_slice_in_dim(drift_now, member * slice_width, slice_width, 1)
        before_piece = prefix(drift_piece, "tm", add_fields, jnp.zeros_like(drift_piece))
        reached = lax.all_gather(
            shortened(before_piece + drift_piece), "tensor", axis=1, tiled=True
        )
        picard_map = noise_start + reached
        residual_rows.append(jnp.mean(jnp.square(picard_map - state_out)))
        state_new = picard_map + mixing[iteration, 0] * (picard_map - previous)
        previous = picard_map
        state_out = state_new
        if iteration + 1 < ITERS:
            state_in = noise_start + from_behind(shortened(state_new - noise_start), "tm", 1)
    return (state_out[None], jnp.stack(residual_rows)[:, None])


def solution(mesh):
    in_specs = (
        P(),
        P(),
        P("tm", None),
        P(None, "tm"),
        P(),
        P(),
        P(),
        P(),
        P(),
        P(),
        P(),
        P(),
        P(),
        P(None, "tensor"),
        P("tensor", None),
        P(),
    )
    out_specs = (P("tm", None, None), P(None, "tm"))
    return jax.shard_map(
        per_device, mesh=mesh, in_specs=in_specs, out_specs=out_specs, check_vma=False
    )
```

profile of v0, /device:TPU:0, one launch (start us, length us, event | category | flops | bytes accessed | tf_op | source)
XLA Modules:
  0.0 339.4 jit_solution(7551914350179567751)
XLA Ops:
  7.3 6.6 %fusion.78 = (f32[1024,384]{1,0:T(8,128)}, f32[1024,384]{1,0:T(8,128)}) fusion(f32[384]{0:T(512)S(1)} %multiply_exponential_fusion), kind=kLoop, calls=%fused_computation.95 | loop fusion | flops 393216 | bytes 3147264 | tf_op jit(solution)/shard_map/sin | solution.py:75
  23.3 4.1 %fusion.135 = f32[1,4608]{1,0:T(1,128)S(1)} fusion(bf16[768,1]{0,1:T(2,128)(2,1)S(1)} %reshape.487, bf16[768,4608]{1,0:T(8,128)(2,1)} %param.27), kind=kOutput, calls=%fused_computation.196 | convolution fusion | flops 7077888 | bytes 7097856 | tf_op jit(solution)/shard_map/dot_general | solution.py:140
  27.6 2.7 convolution_convert_fusion.1
  30.8 3.6 %convolution_convert_fusion.3 = bf16[512,768]{1,0:T(8,128)(2,1)} fusion(bf16[768,768]{1,0:T(8,128)(2,1)} %param.30, f32[512,768]{1,0:T(8,128)} %copy-done.6, f32[768]{0:T(1024)S(1)} %get-tuple-element.196, f32[768]{0:T(1024)S(1)} %get-tuple-element.197, f32[512]{0:T(512)S(1)} %add_rsqrt_fusion.5, f32[512]{0:T(512)S(1)} %broadcast_multiply_fusion.5), kind=kOutput, calls=%fused_computation.105 | convolution fusion | flops 606339072 | bytes 3549184 | tf_op jit(solution)/shard_map/dot_general | solution.py:161
  36.7 8.5 %all-gather.13.cloned.1.call-done = bf16[1024,1536]{1,0:T(8,128)(2,1)} async-done(((bf16[512,1536]{1,0:T(8,128)(2,1)}), bf16[1024,1536]{1,0:T(8,128)(2,1)}) %all-gather.13.cloned.1.call-update) | async-done | bytes 3145744 | tf_op jit(solution)/shard_map/all_gather | solution.py:169
  45.2 3.8 %fusion.128 = (bf16[1,1024,768]{2,1,0:T(8,128)(2,1)}, bf16[1,1024,768]{2,1,0:T(8,128)(2,1)}) fusion(bf16[1,1024,1536]{2,1,0:T(8,128)(2,1)} %bitcast.198), kind=kLoop, calls=%fused_computation.189 | loop fusion | bytes 6291456 | tf_op jit(solution)/shard_map/slice | solution.py:170
  54.2 13.0 %fusion.132 = (f32[12,512]{1,0:T(8,128)S(1)}, f32[12,512,1024]{2,1,0:T(8,128)}) fusion(bf16[512,12,64]{0,2,1:T(8,128)(2,1)} %bitcast.203, bf16[1024,12,64]{0,2,1:T(8,128)(2,1)} %bitcast.199), kind=kOutput, calls=%fused_computation.193 | convolution fusion | flops 824181760 | bytes 27549696 | tf_op jit(solution)/shard_map/sub | solution.py:176
  67.2 10.9 %fusion.90 = bf16[12,64,512]{2,1,0:T(8,128)(2,1)S(1)} fusion(bf16[1024,12,64]{0,2,1:T(8,128)(2,1)} %bitcast.200, f32[12,512,1024]{2,1,0:T(8,128)} %get-tuple-element.240, f32[12,512]{1,0:T(8,128)S(1)} %get-tuple-element.239), kind=kOutput, calls=%fused_computation.103 | convolution fusion | flops 818282496 | bytes 27549696 | tf_op jit(solution)/shard_map/bhqk,bkhd->bqhd/dot_general | solution.py:177
  80.1 10.9 %all-gather.15.cloned.1.call-done = bf16[1024,768]{1,0:T(8,128)(2,1)} async-done(((bf16[512,768]{1,0:T(8,128)(2,1)}), bf16[1024,768]{1,0:T(8,128)(2,1)}) %all-gather.15.cloned.1.call-update) | async-done | bytes 1572880 | tf_op jit(solution)/shard_map/all_gather | solution.py:185
  93.6 9.4 %fusion.86 = bf16[1,1024,768]{2,1,0:T(8,128)(2,1)} fusion(bf16[1536,768]{1,0:T(8,128)(2,1)} %param.34, bf16[768,1536]{1,0:T(8,128)(2,1)} %param.33, bf16[1024,768]{1,0:T(8,128)(2,1)} %all-gather.15.cloned.1.call-done, f32[768]{0:T(1024)S(1)} %get-tuple-element.199, f32[768]{0:T(1024)S(1)} %get-tuple-element.195, f32[1024]{0:T(1024)S(1)} %add_rsqrt_fusion.3, ...), kind=kOutput, calls=%fused_computation.99 | convolution fusion | flops 4851499008 | bytes 7878656 | tf_op jit(solution)/shard_map/dot_general | solution.py:195
  112.4 12.3 %all-reduce.4.cloned.1.call-done = bf16[1,1024,768]{2,1,0:T(8,128)(2,1)} async-done(((bf16[1,1024,768]{2,1,0:T(8,128)(2,1)}), bf16[1,1024,768]{2,1,0:T(8,128)(2,1)}) %all-reduce.4.cloned.1.call-update) | async-done | bytes 1572880 | tf_op jit(solution)/shard_map/psum | solution.py:194
  124.7 2.6 fusion.59
  130.0 44.0 %all-gather.6 = bf16[16,1,8192]{2,1,0:T(2,128)(2,1)S(1)} all-gather(bf16[1,1,8192]{2,1,0:T(2,128)(2,1)S(1)} %get-tuple-element.224), channel_id=4, replica_groups=mesh['tm'=16,'tensor'=2] {'tm'}, dimensions={0}, use_global_device_ids=true | all-gather | bytes 278528 | tf_op jit(solution)/shard_map/all_gather | solution.py:25
  184.6 2.7 convolution_convert_fusion
  187.6 2.6 convolution_convert_fusion.2
  190.5 7.5 %all-gather.17.cloned.1.call-done = bf16[1024,1536]{1,0:T(8,128)(2,1)} async-done(((bf16[512,1536]{1,0:T(8,128)(2,1)}), bf16[1024,1536]{1,0:T(8,128)(2,1)}) %all-gather.17.cloned.1.call-update) | async-done | bytes 3145744 | tf_op jit(solution)/shard_map/all_gather | solution.py:169
  198.0 3.2 fusion.127
  205.4 12.9 %fusion.134 = (f32[12,512]{1,0:T(8,128)S(1)}, f32[12,512,1024]{2,1,0:T(8,128)}) fusion(bf16[512,12,64]{0,2,1:T(8,128)(2,1)S(1)} %bitcast.204, bf16[1024,12,64]{0,2,1:T(8,128)(2,1)} %bitcast.201), kind=kOutput, calls=%fused_computation.195 | convolution fusion | flops 824181760 | bytes 27549696 | tf_op jit(solution)/shard_map/sub | solution.py:176
  218.3 10.9 %fusion.89 = bf16[12,64,512]{2,1,0:T(8,128)(2,1)S(1)} fusion(bf16[1024,12,64]{0,2,1:T(8,128)(2,1)} %bitcast.202, f32[12,512,1024]{2,1,0:T(8,128)} %get-tuple-element.244, f32[12,512]{1,0:T(8,128)S(1)} %get-tuple-element.243), kind=kOutput, calls=%fused_computation.102 | convolution fusion | flops 818282496 | bytes 27549696 | tf_op jit(solution)/shard_map/bhqk,bkhd->bqhd/dot_general | solution.py:177
  231.3 10.8 %all-gather.19.cloned.1.call-done = bf16[1024,768]{1,0:T(8,128)(2,1)} async-done(((bf16[512,768]{1,0:T(8,128)(2,1)}), bf16[1024,768]{1,0:T(8,128)(2,1)}) %all-gather.19.cloned.1.call-update) | async-done | bytes 1572880 | tf_op jit(solution)/shard_map/all_gather | solution.py:185
  244.6 8.9 %fusion.83 = bf16[1,1024,768]{2,1,0:T(8,128)(2,1)} fusion(bf16[1536,768]{1,0:T(8,128)(2,1)} %param.34, bf16[768,1536]{1,0:T(8,128)(2,1)} %param.33, bf16[1024,768]{1,0:T(8,128)(2,1)S(1)} %copy-done.4, f32[1024]{0:T(1024)S(1)} %add_rsqrt_fusion.1, f32[1024]{0:T(1024)S(1)} %broadcast_multiply_fusion.1, f32[768]{0:T(1024)S(1)} %get-tuple-element.199, ...), kind=kOutput, calls=%fused_computation.98 | convolution fusion | flops 4851499008 | bytes 7878656 | tf_op jit(solution)/shard_map/dot_general | solution.py:195
  253.6 21.7 %all-reduce.6.cloned.1.call-done = bf16[1,1024,768]{2,1,0:T(8,128)(2,1)} async-done(((bf16[1,1024,768]{2,1,0:T(8,128)(2,1)}), bf16[1,1024,768]{2,1,0:T(8,128)(2,1)}) %all-reduce.6.cloned.1.call-update) | async-done | bytes 1572880 | tf_op jit(solution)/shard_map/psum | solution.py:194
  280.4 44.0 %all-gather.7 = bf16[16,1,8192]{2,1,0:T(2,128)(2,1)S(1)} all-gather(bf16[1,1,8192]{2,1,0:T(2,128)(2,1)S(1)} %get-tuple-element.220), channel_id=7, replica_groups=mesh['tm'=16,'tensor'=2] {'tm'}, dimensions={0}, use_global_device_ids=true | all-gather | bytes 278528 | tf_op jit(solution)/shard_map/all_gather | solution.py:25
  327.6 2.7 multiply_reduce_fusion.7
  (170 shorter events, 59.5 us)
Async XLA Ops:
  7.2 20.4 %copy-start = (bf16[768,1536]{1,0:T(8,128)(2,1)S(1)}, bf16[768,1536]{1,0:T(8,128)(2,1)}, u32[]{:S(2)}) copy-start(bf16[768,1536]{1,0:T(8,128)(2,1)} %param.31) | copy-start | bytes 7077892
  7.2 6.7 %copy-start.13 = (f32[1,16384]{1,0:T(1,128)S(1)}, f32[1,16384]{1,0:T(1,128)}, u32[]{:S(2)}) copy-start(f32[1,16384]{1,0:T(1,128)} %param.20) | copy-start | bytes 196612
  7.2 7.1 %copy-start.15 = (bf16[16,768]{1,0:T(8,128)(2,1)S(1)}, bf16[16,768]{1,0:T(8,128)(2,1)}, u32[]{:S(2)}) copy-start(bf16[16,768]{1,0:T(8,128)(2,1)} %param.29) | copy-start | bytes 73732
  7.2 38.0 %all-gather.13.cloned.1.call-start = ((), (), s32[]{:S(2)}) async-start(), calls=%async_computation.2 | async-start | bytes 4718592 | tf_op jit(solution)/shard_map/all_gather | solution.py:169
  14.3 3.4 copy-start.17
  14.3 4.8 %copy-start.14 = (bf16[256,768]{1,0:T(8,128)(2,1)S(1)}, bf16[256,768]{1,0:T(8,128)(2,1)}, u32[]{:S(2)}) copy-start(bf16[256,768]{1,0:T(8,128)(2,1)} %param.25) | copy-start | bytes 1179652
  23.3 4.2 %copy-start.7 = (f32[512,768]{1,0:T(8,128)S(1)}, f32[512,768]{1,0:T(8,128)}, u32[]{:S(2)}) copy-start(f32[512,768]{1,0:T(8,128)} %copy-done.6) | copy-start | bytes 4718596
  30.2 60.8 %all-gather.15.cloned.1.call-start = ((), (), s32[]{:S(2)}) async-start(), calls=%async_computation.3 | async-start | bytes 2359296 | tf_op jit(solution)/shard_map/all_gather | solution.py:185
  67.2 10.9 %copy-start.8 = (f32[512,768]{1,0:T(8,128)S(1)}, f32[512,768]{1,0:T(8,128)}, u32[]{:S(2)}) copy-start(f32[512,768]{1,0:T(8,128)} %copy-done.6) | copy-start | bytes 4718596
  67.2 10.9 %copy-start.18 = (bf16[768,768]{1,0:T(8,128)(2,1)S(1)}, bf16[768,768]{1,0:T(8,128)(2,1)}, u32[]{:S(2)}) copy-start(bf16[768,768]{1,0:T(8,128)(2,1)} %param.32) | copy-start | bytes 3538948
  79.9 44.8 %all-reduce.4.cloned.1.call-start = ((), (), s32[]{:S(2)}) async-start(), calls=%async_computation | async-start | bytes 3145728 | tf_op jit(solution)/shard_map/psum | solution.py:194
  91.0 1.9 copy-start.2
  93.6 16.1 %copy-start.16 = (f32[2,1]{0,1:T(1,128)S(1)}, f32[2,1]{0,1:T(1,128)}, u32[]{:S(2)}) copy-start(f32[2,1]{0,1:T(1,128)} %param.23) | copy-start | bytes 28
  103.0 95.0 %all-gather.17.cloned.1.call-start = ((), (), s32[]{:S(2)}) async-start(), calls=%async_computation.4 | async-start | bytes 4718592 | tf_op jit(solution)/shard_map/all_gather | solution.py:169
  124.7 2.6 copy-start.3
  124.7 2.8 copy-start.9
  177.9 3.2 collective-permute-start
  187.3 54.8 %all-gather.19.cloned.1.call-start = ((), (), s32[]{:S(2)}) async-start(), calls=%async_computation.5 | async-start | bytes 2359296 | tf_op jit(solution)/shard_map/all_gather | solution.py:185
  218.3 10.9 %copy-start.11 = (f32[512,768]{1,0:T(8,128)S(1)}, f32[512,768]{1,0:T(8,128)}, u32[]{:S(2)}) copy-start(f32[512,768]{1,0:T(8,128)} %copy-done.10) | copy-start | bytes 4718596
  218.3 10.9 %copy-start.19 = (bf16[768,768]{1,0:T(8,128)(2,1)S(1)}, bf16[768,768]{1,0:T(8,128)(2,1)}, u32[]{:S(2)}) copy-start(bf16[768,768]{1,0:T(8,128)(2,1)} %param.32) | copy-start | bytes 3538948
  231.0 44.3 %all-reduce.6.cloned.1.call-start = ((), (), s32[]{:S(2)}) async-start(), calls=%async_computation.1 | async-start | bytes 3145728 | tf_op jit(solution)/shard_map/psum | solution.py:194
  242.1 1.9 copy-start.4
  275.3 2.1 copy-start.12
  278.8 53.5 %copy-start.1 = (bf16[768,1536]{1,0:T(8,128)(2,1)S(1)}, bf16[768,1536]{1,0:T(8,128)(2,1)}, u32[]{:S(2)}) copy-start(bf16[768,1536]{1,0:T(8,128)(2,1)} %param.31) | copy-start | bytes 7077892
  (4 other events, 4.9 us)
Sparse Core Ops, SparseCore 0:
  30.4 14.8 all-gather.12
  80.0 10.9 all-gather.14
  103.1 21.5 all-reduce.3
  187.4 10.4 all-gather.16
  231.1 10.9 all-gather.18
  253.7 21.5 all-reduce.5
where the time goes:
time: 344 us; the launch traced here: 339 us
  matrix products  96.6 us (28%)
  blocking collectives  91.7 us (27%)
  waiting for transfers between devices  73.7 us (21%)
  other arithmetic  27.8 us (8%)
  local copies, waits for them, and re-layouts  24.7 us (7%)
  between operations  21.3 us (6%)
    all_gather x2, blocking collectives, prefix(): lax.all_gather(array.astype(jnp.bfloat16 if array.dtype == jnp.float32 el...  88 us
    psum x2, waiting for transfers between devices, per_device(): lax.psum(jnp.dot(lifted, down_weight, preferred_element_type=jnp.float32)...  34 us
    sub x2, matrix products, per_device(): attention = jax.nn.softmax(scores, axis=-1).astype(jnp.bfloat16)  25.9 us
    dot_general x2, matrix products, per_device(): jnp.einsum('bhqk,bkhd->bqhd', attention, value_heads, preferred_element_t...  21.8 us
    all_gather x2, waiting for transfers between devices, per_device(): lax.all_gather(hidden.astype(jnp.bfloat16), 'tensor', axis=1, tiled=True)  21.7 us
    dot_general x2, matrix products, per_device(): jnp.dot(lifted, down_weight, preferred_element_type=jnp.float32)  18.3 us
    all_gather x2, waiting for transfers between devices, per_device(): gathered = lax.all_gather(key_value, 'tensor', axis=1, tiled=True)  16 us
    slice x4, local copies, waits for them, and re-layouts, per_device(): key_heads = gathered[:, :, :D].reshape(IMG, SEQ, HEADS, head_dim)  12.2 us
  transfers between devices with their start and end apart: 7, of which 7 were waited for; matrix products, arithmetic and copies ran while one was open for 4% of the time, Pallas kernels for 0%

commit v1 on v0

v1 whole, which is shorter than its diff:
```python
import functools
import math

import jax
import jax.numpy as jnp
from jax import lax
from jax.experimental import pallas as pl
from jax.experimental.pallas import tpu as pltpu
from jax.sharding import PartitionSpec as P

HEAD_DIM = 64
ITERS = 2
PERIOD = 32
norm_eps = 1e-06
plan_steps = 1000
MESH = pl.DeviceIdType.MESH
F32 = jnp.float32
BF16 = jnp.bfloat16
ANY = pl.BlockSpec(memory_space=pl.ANY)
VM = pl.BlockSpec(memory_space=pltpu.VMEM)
SM = pl.BlockSpec(memory_space=pltpu.SMEM)
LIMIT = 56 * 1024 * 1024


def log_table():
    levels = jnp.arange(plan_steps, dtype=jnp.float32)
    beta_values = 0.0001 + (0.02 - 0.0001) * levels / (plan_steps - 1)
    return jnp.log(1.0 - beta_values)


def alpha_at(moments):
    reached = jnp.arange(plan_steps, dtype=jnp.int32)[None, :] <= moments[:, None]
    return jnp.exp(jnp.sum(jnp.where(reached, log_table()[None, :], 0.0), axis=1))


def time_features(moment, half_count):
    freq_rates = jnp.exp(
        -math.log(10000.0) * jnp.arange(half_count, dtype=jnp.float32) / half_count
    )
    angles = moment.astype(jnp.float32) * freq_rates
    return jnp.concatenate([jnp.cos(angles), jnp.sin(angles)])[None, :]


def pick_entry(vector, wanted):
    matches = jnp.arange(vector.shape[0], dtype=jnp.int32) == wanted
    return jnp.sum(jnp.where(matches, vector, 0))


def normed(values):
    center = values - jnp.mean(values, axis=-1, keepdims=True)
    spread = jnp.mean(center * center, axis=-1, keepdims=True)
    return center * lax.rsqrt(spread + norm_eps)


def attention_kernel(
    tile,
    x_ref,
    patch_ref,
    far_sin,
    far_cos,
    near_sin,
    near_cos,
    mod_ref,
    q_hbm,
    kv_hbm,
    out_hbm,
    h_ref,
    kv_s,
    q_s,
    att_s,
    q_w,
    kv_w,
    out_w,
    sems,
):
    rows_own, width = h_ref.shape
    seq = x_ref.shape[1]
    copies = [
        pltpu.make_async_copy(src, dst, sems.at[i])
        for i, (src, dst) in enumerate(((kv_hbm, kv_w), (q_hbm, q_w), (out_hbm, out_w)))
    ]
    for copy in copies:
        copy.start()
    shift, scale, gate = mod_ref[0:1, :], 1.0 + mod_ref[1:2, :], mod_ref[2:3, :]
    groups = tile // PERIOD

    def embed(t):
        rows = pl.ds(pl.multiple_of(t * tile, tile), tile)
        tokens = x_ref[:, rows].astype(BF16)
        hidden = lax.dot_general(
            tokens, patch_ref[...], (((0,), (0,)), ((), ())), preferred_element_type=F32
        )
        far = pl.ds(pl.multiple_of(t * groups, groups), groups)
        fs, fc = far_sin[far, :][:, None, :], far_cos[far, :][:, None, :]
        ns, nc = near_sin[...][None], near_cos[...][None]
        sines = (fs * nc + fc * ns).reshape(tile, width // 2)
        cosines = (fc * nc - fs * ns).reshape(tile, width // 2)
        hidden = hidden + jnp.concatenate([sines, cosines], axis=1)
        return rows, hidden, (normed(hidden) * scale + shift).astype(BF16)

    copies[0].wait()
    copies[1].wait()

    @pl.loop(0, rows_own // tile)
    def _(t):
        rows, hidden, attn_in = embed(t)
        h_ref[rows, :] = hidden
        kv_s[rows, :] = jnp.dot(attn_in, kv_w[...], preferred_element_type=F32).astype(BF16)
        q = jnp.dot(attn_in, q_w[...], preferred_element_type=F32).astype(BF16)
        q_s[rows, :] = q * BF16(1.0 / math.sqrt(HEAD_DIM))

    @pl.loop(rows_own // tile, seq // tile)
    def _(t):
        rows, _, attn_in = embed(t)
        kv_s[rows, :] = jnp.dot(attn_in, kv_w[...], preferred_element_type=F32).astype(BF16)

    pair = 2 * HEAD_DIM
    first = lax.broadcasted_iota(jnp.int32, (tile, pair), 1) < HEAD_DIM

    @pl.loop(0, width // pair)
    def _(hp):
        cols = pl.ds(pl.multiple_of(hp * pair, pair), pair)
        keys = kv_s[:, cols]
        values = kv_s[:, pl.ds(pl.multiple_of(width + hp * pair, pair), pair)]
        for t in range(rows_own // tile):
            rows = slice(t * tile, (t + 1) * tile)
            q2 = q_s[rows, cols]
            outs = []
            for mask in (first, jnp.logical_not(first)):
                s = lax.dot_general(
                    jnp.where(mask, q2, BF16(0)),
                    keys,
                    (((1,), (1,)), ((), ())),
                    preferred_element_type=F32,
                )
                p = jnp.exp(s - jnp.max(s, axis=-1, keepdims=True))
                total = jnp.sum(p, axis=-1, keepdims=True)
                o = jnp.dot(p.astype(BF16), values, preferred_element_type=F32)
                outs.append(o * (1.0 / total))
            att_s[rows, cols] = jnp.where(first, outs[0], outs[1]).astype(BF16)

    copies[2].wait()

    @pl.loop(0, rows_own // tile)
    def _(t):
        rows = pl.ds(pl.multiple_of(t * tile, tile), tile)
        h_ref[rows, :] += gate * jnp.dot(att_s[rows, :], out_w[...], preferred_element_type=F32)


def mlp_kernel(
    tile,
    block,
    coef_ref,
    x_ref,
    h_ref,
    mod_ref,
    final_ref,
    up_a,
    up_b,
    down_a,
    down_b,
    d_ref,
    up_w,
    down_w,
    sems,
):
    rows_own, width = h_ref.shape
    hidden_units = up_w.shape[2]
    copies = []
    for i, (src, dst) in enumerate(
        ((up_a, up_w.at[0]), (down_a, down_w.at[0]), (up_b, up_w.at[1]), (down_b, down_w.at[1]))
    ):
        copy = pltpu.make_async_copy(src, dst, sems.at[i])
        copy.start()
        copies.append(copy)
    shift, scale, gate = mod_ref[3:4, :], 1.0 + mod_ref[4:5, :], mod_ref[5:6, :]
    shift_o, scale_o = mod_ref[6:7, :], 1.0 + mod_ref[7:8, :]
    for copy in copies:
        copy.wait()

    @pl.loop(0, rows_own // tile)
    def _(t):
        rows = pl.ds(pl.multiple_of(t * tile, tile), tile)
        h = h_ref[rows, :]
        x = (normed(h) * scale + shift).astype(BF16)
        total = jnp.zeros((tile, width), F32)
        for half in range(2):
            acc = jnp.zeros((tile, width), F32)
            for j in range(hidden_units // block):
                part = slice(j * block, (j + 1) * block)
                lifted = jnp.dot(x, up_w[half, :, part], preferred_element_type=F32)
                lifted = jax.nn.gelu(lifted, approximate=True).astype(BF16)
                acc = acc + jnp.dot(lifted, down_w[half, part, :], preferred_element_type=F32)
            total = total + acc.astype(BF16).astype(F32)
        h2 = h + gate * total
        final_in = (normed(h2) * scale_o + shift_o).astype(BF16)
        eps = lax.dot_general(
            final_ref[...], final_in, (((1,), (1,)), ((), ())), preferred_element_type=F32
        )
        d_ref[:, rows] = (coef_ref[0] * x_ref[:, rows] + coef_ref[1] * eps).astype(BF16)


def prefix_kernel(
    count,
    d_ref,
    prev_ref,
    now_ref,
    held,
    other_d,
    mine,
    other_sum,
    send_sem,
    recv_sem,
    pair_send,
    pair_recv,
):
    here = lax.axis_index("tm")
    core = lax.axis_index("tensor")
    partner = (here, 1 - core)

    def to(target):
        return pltpu.make_async_remote_copy(
            src_ref=d_ref,
            dst_ref=held.at[here],
            send_sem=send_sem.at[target],
            recv_sem=recv_sem.at[here],
            device_id=(target, core),
            device_id_type=MESH,
        )

    def across(src, dst, slot):
        return pltpu.make_async_remote_copy(
            src_ref=src,
            dst_ref=dst,
            send_sem=pair_send.at[slot],
            recv_sem=pair_recv.at[slot],
            device_id=partner,
            device_id_type=MESH,
        )

    barrier = pltpu.get_barrier_semaphore()
    pl.semaphore_signal(barrier, inc=1, device_id=partner, device_id_type=MESH)

    @pl.loop(0, here)
    def _(j):
        pl.semaphore_signal(barrier, inc=1, device_id=(j, core), device_id_type=MESH)

    pl.semaphore_wait(barrier, count - here)

    @pl.loop(here + 1, count)
    def _(t):
        to(t).start()

    swap = across(d_ref, other_d, 0)
    swap.start()

    def add(j, total):
        pltpu.make_async_remote_copy(
            src_ref=d_ref,
            dst_ref=held.at[j],
            send_sem=send_sem.at[j],
            recv_sem=recv_sem.at[j],
            device_id=partner,
            device_id_type=MESH,
        ).wait_recv()
        return total + held[j].astype(F32)

    before = lax.fori_loop(0, here, add, jnp.zeros(d_ref.shape, F32))
    mine[...] = before.astype(BF16)
    swap_sum = across(mine, other_sum, 1)
    swap_sum.start()
    prev_ref[0] = before
    now_ref[0] = before + d_ref[...].astype(F32)
    swap.wait()
    swap_sum.wait()
    behind = other_sum[...].astype(F32)
    prev_ref[1] = behind
    now_ref[1] = behind + other_d[...].astype(F32)

    @pl.loop(here + 1, count)
    def _(t):
        to(t).wait_send()


def run_attention(x, patch, tables, mods, q_w, kv_w, out_w, rows_own):
    width = q_w.shape[0]
    seq = x.shape[1]
    tile = 256
    flops = 2 * seq * width * 2 * width + 4 * rows_own * width * width + 16 * rows_own * seq * width
    return pl.pallas_call(
        functools.partial(attention_kernel, tile),
        out_shape=jax.ShapeDtypeStruct((rows_own, width), F32),
        in_specs=[VM] * 7 + [ANY] * 3,
        out_specs=VM,
        scratch_shapes=[
            pltpu.VMEM((seq, 2 * width), BF16),
            pltpu.VMEM((rows_own, width), BF16),
            pltpu.VMEM((rows_own, width), BF16),
            pltpu.VMEM(q_w.shape, BF16),
            pltpu.VMEM(kv_w.shape, BF16),
            pltpu.VMEM(out_w.shape, BF16),
            pltpu.SemaphoreType.DMA((3,)),
        ],
        compiler_params=pltpu.CompilerParams(vmem_limit_bytes=LIMIT),
        cost_estimate=pl.CostEstimate(
            flops=flops, bytes_accessed=8_000_000, transcendentals=rows_own * seq * width // 64
        ),
        name="attention",
    )(x, patch, *tables, mods, q_w, kv_w, out_w)


def run_mlp(coefs, x_own, h, mods, final_t, up_a, up_b, down_a, down_b):
    rows_own, width = h.shape
    units = up_a.shape[1]
    return pl.pallas_call(
        functools.partial(mlp_kernel, 256, 512),
        out_shape=jax.ShapeDtypeStruct((final_t.shape[0], rows_own), BF16),
        in_specs=[SM] + [VM] * 4 + [ANY] * 4,
        out_specs=VM,
        scratch_shapes=[
            pltpu.VMEM((2, width, units), BF16),
            pltpu.VMEM((2, units, width), BF16),
            pltpu.SemaphoreType.DMA((4,)),
        ],
        compiler_params=pltpu.CompilerParams(vmem_limit_bytes=LIMIT),
        cost_estimate=pl.CostEstimate(
            flops=8 * rows_own * width * units, bytes_accessed=12_000_000, transcendentals=0
        ),
        name="feed_forward",
    )(coefs, x_own, h, mods, final_t, up_a, up_b, down_a, down_b)


def run_prefix(count, drift):
    part = drift.shape
    both = jax.ShapeDtypeStruct((2,) + part, F32)
    return pl.pallas_call(
        functools.partial(prefix_kernel, count),
        out_shape=(both, both),
        in_specs=[VM],
        out_specs=(VM, VM),
        scratch_shapes=[
            pltpu.VMEM((count,) + part, BF16),
            pltpu.VMEM(part, BF16),
            pltpu.VMEM(part, BF16),
            pltpu.VMEM(part, BF16),
            pltpu.SemaphoreType.DMA((count,)),
            pltpu.SemaphoreType.DMA((count,)),
            pltpu.SemaphoreType.DMA((2,)),
            pltpu.SemaphoreType.DMA((2,)),
        ],
        compiler_params=pltpu.CompilerParams(collective_id=0, has_side_effects=True),
        name="prefix",
    )(drift)


def per_device(
    noise_start,
    timesteps,
    class_labels,
    mixing,
    class_table,
    time_in,
    time_out,
    ada_weight,
    final_ada,
    patch_weight,
    q_weight,
    kv_weight,
    out_weight,
    up_weight,
    down_weight,
    final_weight,
):
    count = lax.axis_size("tm")
    point = lax.axis_index("tm")
    member = lax.axis_index("tensor")
    patch, width = patch_weight.shape
    seq = noise_start.shape[1] // patch
    rows_own = seq // 2
    swap = [(0, 1), (1, 0)]
    up_other = lax.ppermute(up_weight, "tensor", swap)
    down_other = lax.ppermute(down_weight, "tensor", swap)
    mixing_before = lax.ppermute(mixing, "tm", [(i, i + 1) for i in range(count - 1)])

    moments = jnp.stack([pick_entry(timesteps, point), pick_entry(timesteps, point + 1)])
    alphas = alpha_at(moments)
    keep_coef = jnp.sqrt(alphas[1] / alphas[0])
    noise_coef = jnp.sqrt(1.0 - alphas[1]) - jnp.sqrt(alphas[1] * (1.0 - alphas[0]) / alphas[0])
    coefs = jnp.stack([keep_coef - 1.0, noise_coef])

    features = time_features(moments[0], time_in.shape[0] // 2).astype(BF16)
    time_hidden = jax.nn.silu(jnp.dot(features, time_in, preferred_element_type=F32)).astype(BF16)
    time_embed = jnp.dot(time_hidden, time_out, preferred_element_type=F32)
    classes = lax.dynamic_slice_in_dim(class_table, class_labels[0, 0], 1, 0).astype(F32)
    cond = jax.nn.silu(time_embed + classes).astype(BF16)
    modul = jnp.dot(cond, ada_weight, preferred_element_type=F32)
    final_mod = jnp.dot(cond, final_ada, preferred_element_type=F32)
    mods = jnp.concatenate([modul, final_mod], axis=1).reshape(8, width)

    half_width = width // 2
    rates = jnp.exp(-math.log(10000.0) * jnp.arange(half_width, dtype=F32) / half_width)
    near = jnp.arange(PERIOD, dtype=F32)[:, None] * rates[None]
    spans = seq // PERIOD
    turn = (jnp.arange(spans, dtype=jnp.int32) + member * (spans // 2)) % spans
    far = (turn * PERIOD).astype(F32)[:, None] * rates[None]
    tables = (jnp.sin(far), jnp.cos(far), jnp.sin(near), jnp.cos(near))

    plain = noise_start.reshape(seq, patch).T.reshape(patch, 2, rows_own)
    swapped = plain[:, ::-1]
    noise = jnp.where(member == 0, plain, swapped).reshape(patch, seq)
    halves = jnp.stack([noise[:, :rows_own], noise[:, rows_own:]])
    final_t = final_weight.T

    def denoise(x):
        h = run_attention(
            x, patch_weight, tables, mods, q_weight, kv_weight, out_weight, rows_own
        )
        drift = run_mlp(
            coefs, x[:, :rows_own], h, mods, final_t, up_weight, up_other, down_weight, down_other
        )
        return run_prefix(count, drift)

    before, sums = denoise(noise)
    residuals = [jnp.mean(jnp.square(sums))]
    state = halves + (1.0 + mixing[0, 0]) * sums
    x = halves + (1.0 + mixing_before[0, 0]) * before
    _, sums_next = denoise(jnp.concatenate([x[0], x[1]], axis=1))
    picard = halves + sums_next
    residuals.append(jnp.mean(jnp.square(picard - state)))
    state = picard + mixing[1, 0] * (sums_next - sums)
    ordered = jnp.where(member == 0, state, state[::-1])
    states = ordered.transpose(0, 2, 1).reshape(1, 1, seq * patch)
    return (states, jnp.stack(residuals)[:, None])


def solution(mesh):
    in_specs = (
        P(),
        P(),
        P("tm", None),
        P(None, "tm"),
        P(),
        P(),
        P(),
        P(),
        P(),
        P(),
        P(),
        P(),
        P(),
        P(None, "tensor"),
        P("tensor", None),
        P(),
    )
    out_specs = (P("tm", None, None), P(None, "tm"))
    return jax.shard_map(
        per_device, mesh=mesh, in_specs=in_specs, out_specs=out_specs, check_vma=False
    )
```

time: 344 us -> 135 us (0.39)
  Pallas kernels: 0 us -> 97.5 us
  blocking collectives: 91.7 us -> 0 us
  matrix products: 96.6 us -> 7.19 us
  waiting for transfers between devices: 73.7 us -> 0.01 us
  local copies, waits for them, and re-layouts: 24.7 us -> 4.63 us
  other arithmetic: 27.8 us -> 9.62 us
  between operations: 21.3 us -> 7.98 us
    pallas_call x0 -> x6, Pallas kernels: none -> 97.5 us  [the longest x2 46.4 us: run_attention(): pl.pallas_call(functools.partial(attention_kernel, tile), out_shape=jax.S...]
    all_gather x4 -> x0, blocking collectives: 91.7 us -> none  [the longest x2 88 us: prefix(): lax.all_gather(array.astype(jnp.bfloat16 if array.dtype == jnp.float32 el...]
    dot_general x19 -> x4, matrix products: 70.7 us -> 7.19 us  [the longest x1 4.02 us: per_device(): modul = jnp.dot(cond, ada_weight, preferred_element_type=F32)]
    all_gather x4 -> x0, waiting for transfers between devices: 37.7 us -> none  [the longest x2 21.7 us: per_device(): lax.all_gather(hidden.astype(jnp.bfloat16), 'tensor', axis=1, tiled=True)]
    psum x2 -> x0, waiting for transfers between devices: 34 us -> none  [per_device(): lax.psum(jnp.dot(lifted, down_weight, preferred_element_type=jnp.float32)...]
    sub x2 -> x0, matrix products: 25.9 us -> none  [per_device(): attention = jax.nn.softmax(scores, axis=-1).astype(jnp.bfloat16)]
    slice x8 -> x1, local copies, waits for them, and re-layouts: 17.1 us -> 0.6 us  [per_device(): state = halves + (1.0 + mixing[0, 0]) * sums]
    reduce_sum x12 -> x2, other arithmetic: 14.8 us -> 2.29 us  [the longest x1 2.1 us: per_device(): residuals = [jnp.mean(jnp.square(sums))]]
  transfers between devices with their start and end apart: 7 -> 3, of which waited for: 7 -> 0; matrix products, arithmetic and copies ran while one was open for 4% -> 12% of each run, Pallas kernels for 0% -> 17%
where the time goes in v1:
time: 135 us; the launch traced here: 132 us
  Pallas kernels  97.5 us (72%)
  other arithmetic  9.62 us (7%)
  between operations  7.98 us (6%)
  matrix products  7.19 us (5%)
  starting transfers between devices  5.57 us (4%)
  local copies, waits for them, and re-layouts  4.63 us (3%)
    pallas_call x2, Pallas kernels, run_attention(): pl.pallas_call(functools.partial(attention_kernel, tile), out_shape=jax.S...  46.4 us
    pallas_call x2, Pallas kernels, run_mlp(): pl.pallas_call(functools.partial(mlp_kernel, 256, 512), out_shape=jax.Sha...  26.8 us
    pallas_call x2, Pallas kernels, run_prefix(): pl.pallas_call(functools.partial(prefix_kernel, count), out_shape=(both,...  24.3 us
    ppermute x1, starting transfers between devices, per_device(): lax.ppermute(mixing, 'tm', [(i, i + 1) for i in range(count - 1)])  4.93 us
    dot_general x1, matrix products, per_device(): modul = jnp.dot(cond, ada_weight, preferred_element_type=F32)  4.02 us
  transfers between devices with their start and end apart: 3, of which 0 were waited for; matrix products, arithmetic and copies ran while one was open for 12% of the time, Pallas kernels for 17%

profile of v1, /device:TPU:0, one launch (start us, length us, event | category | flops | bytes accessed | tf_op | source)
XLA Modules:
  0.0 132.5 jit_solution(879800672218714658)
XLA Ops:
  1.3 4.9 %collective-permute-start = (f32[2,1]{0,1:T(1,128)}, f32[2,1]{0,1:T(1,128)S(1)}, u32[]{:S(2)}, u32[]{:S(2)}) collective-permute-start(f32[2,1]{0,1:T(1,128)} %param.19), channel_id=1, source_target_pairs={{0,2},{2,4},{4,6},{6,8},{8,10},{10,12},{12,14},{14,16},{16,18},{18... | collective-permute-start | bytes 32 | tf_op jit(solution)/shard_map/ppermute | solution.py:383
  6.2 1.3 fusion.11
  7.5 1.4 %pad_add_fusion = s32[2]{0:T(128)S(1)} fusion(s32[1]{0:T(128)} %bitcast.6, s32[1]{0:T(128)} %bitcast.5), kind=kLoop, calls=%fused_computation.43 | loop fusion | flops 2 | bytes 16 | tf_op jit(solution)/shard_map/stack | solution.py:385
  9.1 0.6 fusion.17
  14.2 1.2 convolution_reduce_fusion
  16.1 1.6 %divide_multiply_fusion = bf16[1,768]{1,0:T(2,128)(2,1)S(1)} fusion(bf16[768,1]{0,1:T(2,128)(2,1)S(1)} %reshape.85, bf16[768,768]{1,0:T(8,128)(2,1)} %param.22, bf16[1000,768]{1,0:T(8,128)(2,1)} %param.20, s32[]{:T(128)S(6)} %select_n.48), kind=kOutput, calls=%fused_computation.25 | convolution fusion | flops 1185024 | bytes 1184260 | tf_op jit(solution)/shard_map/dot_general | solution.py:393
  17.6 4.0 %fusion.7 = f32[1,4608]{1,0:T(1,128)S(1)} fusion(bf16[768,4608]{1,0:T(8,128)(2,1)} %param.23, bf16[1,768]{1,0:T(2,128)(2,1)S(1)} %divide_multiply_fusion), kind=kOutput, calls=%fused_computation.28 | convolution fusion | flops 7077888 | bytes 7097856 | tf_op jit(solution)/shard_map/dot_general | solution.py:396
  22.2 0.6 reshape.81.mod_ref
  23.3 0.8 reduce.9
  24.8 0.6 fusion.16
  26.1 0.6 pad_maximum_fusion.2.coef_ref
  26.6 0.6 slice_bitcast_fusion.3
  27.3 1.0 fusion.1
  28.3 23.2 %attention.2.h_ref = f32[512,768]{1,0:T(8,128)} custom-call(f32[16,1024]{1,0:T(8,128)} %bitcast.53, bf16[16,768]{1,0:T(8,128)(2,1)} %patch_ref.3, f32[32,384]{1,0:T(8,128)} %get-tuple-element.22.far_sin, f32[32,384]{1,0:T(8,128)} %get-tuple-element.23.far_cos, f32[32,384]{1,0:T(8,128)} %get-tuple-element.21.near_sin, f32[32,384]{1,0:T(8,128)} %get-tuple-element.20.near_cos, ...), custom_call_target="tpu_custom_call" | custom-call | flops 10066329600 | bytes 8000000 | tf_op jit(solution)/shard_map/attention/pallas_call | solution.py:290
  51.5 13.4 %feed_forward.2.d_ref = bf16[16,512]{1,0:T(8,128)(2,1)} custom-call(f32[2]{0:T(128)} %pad_maximum_fusion.2.coef_ref, f32[16,512]{1,0:T(8,128)} %get-tuple-element.17.x_ref, f32[512,768]{1,0:T(8,128)} %attention.2.h_ref, f32[8,768]{1,0:T(8,128)} %reshape.81.mod_ref, bf16[16,768]{1,0:T(8,128)(2,1)} %bitcast.54, bf16[768,1536]{1,0:T(8,128)(2,1)} %up_a.3, ...), custom_call_target="tpu_custom_call" | custom-call | flops 4831838208 | bytes 12000000 | tf_op jit(solution)/shard_map/feed_forward/pallas_call | solution.py:315
  64.9 10.3 %prefix.2 = (f32[2,16,512]{2,1,0:T(8,128)}, f32[2,16,512]{2,1,0:T(8,128)}) custom-call(bf16[16,512]{1,0:T(8,128)(2,1)} %feed_forward.2.d_ref), custom_call_target="tpu_custom_call" | custom-call | tf_op jit(solution)/shard_map/prefix/pallas_call | solution.py:336
  75.2 0.9 multiply_add_fusion.1
  76.1 0.6 pad_maximum_fusion.1.x_ref
  76.7 23.2 %attention.3.h_ref = f32[512,768]{1,0:T(8,128)} custom-call(f32[16,1024]{1,0:T(8,128)} %pad_maximum_fusion.1.x_ref, bf16[16,768]{1,0:T(8,128)(2,1)} %patch_ref.3, f32[32,384]{1,0:T(8,128)} %get-tuple-element.22.far_sin, f32[32,384]{1,0:T(8,128)} %get-tuple-element.23.far_cos, f32[32,384]{1,0:T(8,128)} %get-tuple-element.21.near_sin, ...), custom_call_target="tpu_custom_call" | custom-call | flops 10066329600 | bytes 8000000 | tf_op jit(solution)/shard_map/attention/pallas_call | solution.py:290
  99.9 13.4 %feed_forward.3.d_ref = bf16[16,512]{1,0:T(8,128)(2,1)} custom-call(f32[2]{0:T(128)} %pad_maximum_fusion.2.coef_ref, f32[16,512]{1,0:T(8,128)} %copy-done.2, f32[512,768]{1,0:T(8,128)} %attention.3.h_ref, f32[8,768]{1,0:T(8,128)} %reshape.81.mod_ref, bf16[16,768]{1,0:T(8,128)(2,1)} %bitcast.55, bf16[768,1536]{1,0:T(8,128)(2,1)} %up_a.3, ...), custom_call_target="tpu_custom_call" | custom-call | flops 4831838208 | bytes 12000000 | tf_op jit(solution)/shard_map/feed_forward/pallas_call | solution.py:315
  113.3 14.1 %prefix.3 = (f32[2,16,512]{2,1,0:T(8,128)}, f32[2,16,512]{2,1,0:T(8,128)}) custom-call(bf16[16,512]{1,0:T(8,128)(2,1)} %feed_forward.3.d_ref), custom_call_target="tpu_custom_call" | custom-call | tf_op jit(solution)/shard_map/prefix/pallas_call | solution.py:336
  127.4 2.1 %multiply_reduce_fusion.1 = (f32[]{:T(128)}, f32[]{:T(128)}, f32[2,16,512]{2,1,0:T(8,128)S(1)}) fusion(f32[2,16,512]{2,1,0:T(8,128)S(1)} %copy-done.4, f32[]{:T(128)} %bitcast.19, f32[2,16,512]{2,1,0:T(8,128)} %get-tuple-element.6, f32[1,16,512]{2,1,0:T(8,128)S(1)} %get-tuple-element.16, f32[1,16,512]{2,1,0:T(8,128)S(1)} %get-tuple-element.15, f32[]{:T(128)} %bitcast.16), kind=kLoop, calls=%fused_computation.9 | loop fusion | flops 196606 | bytes 262160 | tf_op jit(solution)/shard_map/reduce_sum | solution.py:424
  131.0 0.9 reshape.82
  131.9 0.6 maximum_bitcast_fusion
  (38 shorter events, 2.9 us)
Async XLA Ops:
  0.6 21.0 %copy-start = (bf16[768,1536]{1,0:T(8,128)(2,1)S(1)}, bf16[768,1536]{1,0:T(8,128)(2,1)}, u32[]{:S(2)}) copy-start(bf16[768,1536]{1,0:T(8,128)(2,1)} %param.24) | copy-start | bytes 7077892
  0.6 50.9 %collective-permute-start.1 = (bf16[768,1536]{1,0:T(8,128)(2,1)}, bf16[768,1536]{1,0:T(8,128)(2,1)}, u32[]{:S(2)}, u32[]{:S(2)}) collective-permute-start(bf16[768,1536]{1,0:T(8,128)(2,1)} %up_a.3), channel_id=1, source_target_pairs={{0,1},{1,0},{2,3},{3,2},{4,5},{5,4},{6,7},{7,6},{8,9},{9,8},{10,11... | collective-permute-start | bytes 7077896 | tf_op jit(solution)/shard_map/ppermute | solution.py:381
  1.2 50.3 %collective-permute-start.2 = (bf16[1536,768]{1,0:T(8,128)(2,1)}, bf16[1536,768]{1,0:T(8,128)(2,1)}, u32[]{:S(2)}, u32[]{:S(2)}) collective-permute-start(bf16[1536,768]{1,0:T(8,128)(2,1)} %down_a.3), channel_id=1, source_target_pairs={{0,1},{1,0},{2,3},{3,2},{4,5},{5,4},{6,7},{7,6},{8,9},{9,8},{10,11... | collective-permute-start | bytes 7077896 | tf_op jit(solution)/shard_map/ppermute | solution.py:382
  1.3 50.2 %collective-permute-start = (f32[2,1]{0,1:T(1,128)}, f32[2,1]{0,1:T(1,128)S(1)}, u32[]{:S(2)}, u32[]{:S(2)}) collective-permute-start(f32[2,1]{0,1:T(1,128)} %param.19), channel_id=1, source_target_pairs={{0,2},{2,4},{4,6},{6,8},{8,10},{10,12},{12,14},{14,16},{16,18},{18... | collective-permute-start | bytes 32 | tf_op jit(solution)/shard_map/ppermute | solution.py:383
  21.7 1.6 %copy-start.3 = (f32[1,16384]{1,0:T(1,128)S(1)}, f32[1,16384]{1,0:T(1,128)}, u32[]{:S(2)}) copy-start(f32[1,16384]{1,0:T(1,128)} %param.16) | copy-start | bytes 196612
  21.7 3.1 %copy-start.5 = (f32[2,1]{0,1:T(1,128)S(1)}, f32[2,1]{0,1:T(1,128)}, u32[]{:S(2)}) copy-start(f32[2,1]{0,1:T(1,128)} %param.19) | copy-start | bytes 28
  24.8 3.5 %copy-start.1 = (f32[2,8,2,512]{3,1,2,0:T(8,128)}, f32[2,8,2,512]{3,1,2,0:T(8,128)S(1)}, u32[]{:S(2)}) copy-start(f32[2,8,2,512]{3,1,2,0:T(8,128)S(1)} %copy.25) | copy-start | bytes 196612
  76.1 23.9 %copy-start.2 = (f32[16,512]{1,0:T(8,128)}, f32[16,512]{1,0:T(8,128)S(1)}, u32[]{:S(2)}) copy-start(f32[16,512]{1,0:T(8,128)S(1)} %get-tuple-element.14.x_ref) | copy-start | bytes 98308
  99.9 27.5 %copy-start.4 = (f32[2,16,512]{2,1,0:T(8,128)S(1)}, f32[2,16,512]{2,1,0:T(8,128)}, u32[]{:S(2)}) copy-start(f32[2,16,512]{2,1,0:T(8,128)} %get-tuple-element.7) | copy-start | bytes 196612

commit v2 on v1

v2 whole, which is shorter than its diff:
```python
import functools
import math

import jax
import jax.numpy as jnp
from jax import lax
from jax.experimental import pallas as pl
from jax.experimental.pallas import tpu as pltpu
from jax.sharding import PartitionSpec as P
import numpy as np

HEAD_DIM = 64
ITERS = 2
PERIOD = 32
norm_eps = 1e-06
plan_steps = 1000
MESH = pl.DeviceIdType.MESH
F32 = jnp.float32
BF16 = jnp.bfloat16
ANY = pl.BlockSpec(memory_space=pl.ANY)
VM = pl.BlockSpec(memory_space=pltpu.VMEM)
SM = pl.BlockSpec(memory_space=pltpu.SMEM)
LIMIT = 56 * 1024 * 1024


def normed(values):
    center = values - jnp.mean(values, axis=-1, keepdims=True)
    spread = jnp.mean(center * center, axis=-1, keepdims=True)
    return center * lax.rsqrt(spread + norm_eps)


def attention_kernel(
    tile,
    x_ref,
    patch_ref,
    far_sin,
    far_cos,
    near_sin,
    near_cos,
    mod_ref,
    q_hbm,
    kv_hbm,
    out_hbm,
    h_ref,
    kv_s,
    q_s,
    att_s,
    q_w,
    kv_w,
    out_w,
    sems,
):
    rows_own, width = h_ref.shape
    seq = x_ref.shape[1]
    copies = [
        pltpu.make_async_copy(src, dst, sems.at[i])
        for i, (src, dst) in enumerate(((kv_hbm, kv_w), (q_hbm, q_w), (out_hbm, out_w)))
    ]
    for copy in copies:
        copy.start()
    shift, scale, gate = mod_ref[0:1, :], 1.0 + mod_ref[1:2, :], mod_ref[2:3, :]
    groups = tile // PERIOD
    spans = far_sin.shape[0]
    member = lax.axis_index("tensor")

    def embed(t):
        rows = pl.ds(pl.multiple_of(t * tile, tile), tile)
        tokens = x_ref[:, rows].astype(BF16)
        hidden = lax.dot_general(
            tokens, patch_ref[...], (((0,), (0,)), ((), ())), preferred_element_type=F32
        )
        turn = lax.rem(t * groups + member * (spans // 2), spans)
        far = pl.ds(pl.multiple_of(turn, groups), groups)
        fs, fc = far_sin[far, :][:, None, :], far_cos[far, :][:, None, :]
        ns, nc = near_sin[...][None], near_cos[...][None]
        sines = (fs * nc + fc * ns).reshape(tile, width // 2)
        cosines = (fc * nc - fs * ns).reshape(tile, width // 2)
        hidden = hidden + jnp.concatenate([sines, cosines], axis=1)
        return rows, hidden, (normed(hidden) * scale + shift).astype(BF16)

    copies[0].wait()
    copies[1].wait()

    @pl.loop(0, rows_own // tile)
    def _(t):
        rows, hidden, attn_in = embed(t)
        h_ref[rows, :] = hidden
        kv_s[rows, :] = jnp.dot(attn_in, kv_w[...], preferred_element_type=F32).astype(BF16)
        q = jnp.dot(attn_in, q_w[...], preferred_element_type=F32).astype(BF16)
        q_s[rows, :] = q * BF16(1.0 / math.sqrt(HEAD_DIM))

    @pl.loop(rows_own // tile, seq // tile)
    def _(t):
        rows, _, attn_in = embed(t)
        kv_s[rows, :] = jnp.dot(attn_in, kv_w[...], preferred_element_type=F32).astype(BF16)

    pair = 2 * HEAD_DIM
    first = lax.broadcasted_iota(jnp.int32, (tile, pair), 1) < HEAD_DIM

    @pl.loop(0, width // pair)
    def _(hp):
        cols = pl.ds(pl.multiple_of(hp * pair, pair), pair)
        keys = kv_s[:, cols]
        values = kv_s[:, pl.ds(pl.multiple_of(width + hp * pair, pair), pair)]
        for t in range(rows_own // tile):
            rows = slice(t * tile, (t + 1) * tile)
            q2 = q_s[rows, cols]
            outs = []
            for mask in (first, jnp.logical_not(first)):
                s = lax.dot_general(
                    jnp.where(mask, q2, BF16(0)),
                    keys,
                    (((1,), (1,)), ((), ())),
                    preferred_element_type=F32,
                )
                p = jnp.exp(s - jnp.max(s, axis=-1, keepdims=True))
                total = jnp.sum(p, axis=-1, keepdims=True)
                o = jnp.dot(p.astype(BF16), values, preferred_element_type=F32)
                outs.append(o * (1.0 / total))
            att_s[rows, cols] = jnp.where(first, outs[0], outs[1]).astype(BF16)

    copies[2].wait()

    @pl.loop(0, rows_own // tile)
    def _(t):
        rows = pl.ds(pl.multiple_of(t * tile, tile), tile)
        h_ref[rows, :] += gate * jnp.dot(att_s[rows, :], out_w[...], preferred_element_type=F32)


def mlp_kernel(
    tile,
    block,
    coef_ref,
    x_ref,
    h_ref,
    mod_ref,
    final_ref,
    up_a,
    up_b,
    down_a,
    down_b,
    d_ref,
    in_s,
    sum_s,
    up_w,
    down_w,
    sems,
):
    rows_own, width = h_ref.shape
    hidden_units = up_w.shape[2]
    copies = []
    for i, (src, dst) in enumerate(
        ((up_a, up_w.at[0]), (down_a, down_w.at[0]), (up_b, up_w.at[1]), (down_b, down_w.at[1]))
    ):
        copy = pltpu.make_async_copy(src, dst, sems.at[i])
        copy.start()
        copies.append(copy)
    shift, scale, gate = mod_ref[3:4, :], 1.0 + mod_ref[4:5, :], mod_ref[5:6, :]
    shift_o, scale_o = mod_ref[6:7, :], 1.0 + mod_ref[7:8, :]
    keep, noise = coef_ref[0:1, 0:1], coef_ref[1:2, 0:1]
    tiles = rows_own // tile

    def rows_of(t):
        return pl.ds(pl.multiple_of(t * tile, tile), tile)

    @pl.loop(0, tiles)
    def _(t):
        in_s[rows_of(t), :] = (normed(h_ref[rows_of(t), :]) * scale + shift).astype(BF16)

    for half in range(2):
        copies[2 * half].wait()
        copies[2 * half + 1].wait()

        @pl.loop(0, tiles)
        def _(t):
            rows = rows_of(t)
            x = in_s[rows, :]
            acc = jnp.zeros((tile, width), F32)
            for j in range(hidden_units // block):
                part = slice(j * block, (j + 1) * block)
                lifted = jnp.dot(x, up_w[half, :, part], preferred_element_type=F32)
                lifted = jax.nn.gelu(lifted, approximate=True).astype(BF16)
                acc = acc + jnp.dot(lifted, down_w[half, part, :], preferred_element_type=F32)
            acc = acc.astype(BF16).astype(F32)
            if half == 0:
                sum_s[rows, :] = acc
            else:
                h2 = h_ref[rows, :] + gate * (sum_s[rows, :] + acc)
                final_in = (normed(h2) * scale_o + shift_o).astype(BF16)
                eps = lax.dot_general(
                    final_ref[...], final_in, (((1,), (1,)), ((), ())), preferred_element_type=F32
                )
                d_ref[:, rows] = (keep * x_ref[:, rows] + noise * eps).astype(BF16)


def setup_kernel(
    times_ref,
    label_ref,
    noise_ref,
    mixing_ref,
    table_hbm,
    in_hbm,
    out_hbm,
    ada_hbm,
    final_hbm,
    mod_ref,
    coef_ref,
    mix_ref,
    halves_ref,
    x_ref,
    rows_v,
    in_v,
    out_v,
    ada_v,
    final_v,
    sems,
):
    here = lax.axis_index("tm")
    member = lax.axis_index("tensor")
    label = label_ref[0, 0]
    width = mod_ref.shape[1]
    base = pl.multiple_of(label // 8 * 8, 8)
    copies = []

    def begin(src, dst):
        copy = pltpu.make_async_copy(src, dst, sems.at[len(copies)])
        copy.start()
        copies.append(copy)

    begin(in_hbm, in_v)
    begin(out_hbm, out_v)
    begin(table_hbm.at[pl.ds(base, 8), :], rows_v)
    parts = []
    for src, dst in ((ada_hbm, ada_v), (final_hbm, final_v)):
        for j in range(src.shape[1] // width):
            cols = slice(j * width, (j + 1) * width)
            begin(src.at[:, cols], dst.at[:, cols])
            parts.append(dst.at[:, cols])

    level = lax.broadcasted_iota(jnp.int32, (8, 128), 0) * 128
    level = level + lax.broadcasted_iota(jnp.int32, (8, 128), 1)
    beta = 0.0001 + (0.02 - 0.0001) * level.astype(F32) / (plan_steps - 1)
    logs = jnp.log(1.0 - beta)
    now = times_ref[here]

    def alpha(moment):
        kept = jnp.where(level <= moment, logs, 0.0)
        total = jnp.sum(jnp.sum(kept, axis=1, keepdims=True), axis=0, keepdims=True)
        return jnp.exp(total)

    before, after = alpha(now), alpha(times_ref[here + 1])
    keep = jnp.sqrt(after / before) - 1.0
    noise = jnp.sqrt(1.0 - after) - jnp.sqrt(after * (1.0 - before) / before)
    coef_ref[0:1, :] = jnp.broadcast_to(keep, (1, 128))
    coef_ref[1:2, :] = jnp.broadcast_to(noise, (1, 128))
    coef_ref[2:8, :] = jnp.zeros((6, 128), F32)
    mix_ref[0:2, :] = jnp.broadcast_to(mixing_ref[...], (2, 128))
    mix_ref[2:8, :] = jnp.zeros((6, 128), F32)

    plain = noise_ref[...]
    half = plain.shape[1] // 2
    left, right = plain[:, :half], plain[:, half:]
    first = member == 0
    own, other = jnp.where(first, left, right), jnp.where(first, right, left)
    halves_ref[0] = own
    halves_ref[1] = other
    x_ref[:, :half] = own
    x_ref[:, half:] = other

    count = in_v.shape[0] // 2
    lane = lax.broadcasted_iota(jnp.int32, (8, count), 1).astype(F32)
    angle = now.astype(F32) * jnp.exp(-math.log(10000.0) * lane / count)
    features = jnp.concatenate([jnp.cos(angle), jnp.sin(angle)], axis=1).astype(BF16)
    copies[0].wait()
    hidden = jax.nn.silu(jnp.dot(features, in_v[...], preferred_element_type=F32)).astype(BF16)
    copies[1].wait()
    embed = jnp.dot(hidden, out_v[...], preferred_element_type=F32)
    copies[2].wait()
    picked = lax.broadcasted_iota(jnp.int32, (8, width), 0) == label - base
    entry = jnp.sum(jnp.where(picked, rows_v[...].astype(F32), 0.0), axis=0, keepdims=True)
    cond = jax.nn.silu(embed + entry).astype(BF16)
    for j, part in enumerate(parts):
        copies[3 + j].wait()
        mod_ref[j : j + 1, :] = jnp.dot(cond, part[...], preferred_element_type=F32)[0:1, :]


def prefix_kernel(
    count,
    inner,
    last,
    d_ref,
    noise_ref,
    mix_ref,
    *rest,
):
    if last:
        sums_in, state_ref, res_ref, *rest = rest
    else:
        sums_out, x_ref, res_ref, *rest = rest
    held, totals, mine, mix_in, send_a, recv_a, send_b, recv_b, send_m, recv_m = rest
    here = lax.axis_index("tm")
    core = lax.axis_index("tensor")
    outer = count // inner
    group, place = here // inner, here % inner
    start = group * inner

    def copy(src, dst, send, recv, target, target_core):
        return pltpu.make_async_remote_copy(
            src_ref=src,
            dst_ref=dst,
            send_sem=send,
            recv_sem=recv,
            device_id=(target, target_core),
            device_id_type=MESH,
        )

    def inside(i, c):
        return copy(
            d_ref, held.at[place, core], send_a.at[i, c], recv_a.at[place, core], start + i, c
        )

    def onward(g, c):
        return copy(
            mine,
            totals.at[group, core],
            send_b.at[g, c],
            recv_b.at[group, core],
            g * inner + place,
            c,
        )

    def neighbour():
        return copy(mix_ref, mix_in, send_m.at[0], recv_m.at[0], here + 1, core)

    barrier = pltpu.get_barrier_semaphore()

    def greet(target, c):
        pl.semaphore_signal(barrier, inc=1, device_id=(target, c), device_id_type=MESH)

    def others(act):
        act(place, 1 - core)

        @pl.loop(1, inner)
        def _(step):
            i = lax.rem(place + step, inner)
            act(i, 0)
            act(i, 1)

    others(lambda i, c: greet(start + i, c))

    @pl.loop(0, group)
    def _(g):
        greet(g * inner + place, 0)
        greet(g * inner + place, 1)

    waits = 2 * inner - 1 + 2 * (outer - 1 - group)
    if not last:

        @pl.when(here > 0)
        def _():
            greet(here - 1, core)

        waits = waits + jnp.where(here < count - 1, 1, 0)
    pl.semaphore_wait(barrier, waits)

    others(lambda i, c: inside(i, c).start())
    if not last:

        @pl.when(here < count - 1)
        def _():
            neighbour().start()

        @pl.when(here == 0)
        def _():
            mix_in[...] = jnp.zeros_like(mix_in)

    held[place, core] = d_ref[...]

    def arrive_inside(i, c):
        copy(
            d_ref, held.at[i, c], send_a.at[i, c], recv_a.at[i, c], start + i, c
        ).wait_recv()

    others(arrive_inside)
    total = jnp.zeros(d_ref.shape, F32)
    for i in range(inner):
        total = total + held[i, core].astype(F32)
    mine[...] = total.astype(BF16)

    @pl.loop(group + 1, outer)
    def _(g):
        onward(g, 0).start()
        onward(g, 1).start()

    def partial(c):
        def add(i, acc):
            return acc + held[i, c].astype(F32)

        return lax.fori_loop(0, place, add, jnp.zeros(d_ref.shape, F32))

    before = [partial(core), partial(1 - core)]

    @pl.loop(0, group)
    def _(g):
        for c in range(2):
            copy(
                mine,
                totals.at[g, c],
                send_b.at[g, c],
                recv_b.at[g, c],
                g * inner + place,
                c,
            ).wait_recv()

    def gather(c, acc):
        return lax.fori_loop(0, group, lambda g, a: a + totals[g, c].astype(F32), acc)

    before = [gather(core, before[0]), gather(1 - core, before[1])]
    own = held[place, core].astype(F32)
    other = held[place, 1 - core].astype(F32)
    sums = [before[0] + own, before[1] + other]
    noise = [noise_ref[0], noise_ref[1]]
    half = d_ref.shape[1]
    scale = 1.0 / (2 * d_ref.shape[0] * half)

    def mean_square(values):
        total = sum(v * v for v in values)
        total = jnp.sum(jnp.sum(total, axis=1, keepdims=True), axis=0, keepdims=True)
        return jnp.broadcast_to(total * scale, res_ref.shape)

    mix = mix_ref[0:1, 0:1]
    if last:
        old = [sums_in[0], sums_in[1]]
        state = [n + (1.0 + mix) * o for n, o in zip(noise, old)]
        picard = [n + s for n, s in zip(noise, sums)]
        res_ref[...] = mean_square([g - s for g, s in zip(picard, state)])
        mix = mix_ref[1:2, 0:1]
        new = [g + mix * (s - o) for g, s, o in zip(picard, sums, old)]
        first = core == 0
        state_ref[:, :half] = jnp.where(first, new[0], new[1])
        state_ref[:, half:] = jnp.where(first, new[1], new[0])
    else:
        sums_out[0] = sums[0]
        sums_out[1] = sums[1]
        res_ref[...] = mean_square(sums)

        @pl.when(here > 0)
        def _():
            copy(mix_ref, mix_in, send_m.at[0], recv_m.at[0], here - 1, core).wait_recv()

        mix = 1.0 + mix_in[0:1, 0:1]
        x_ref[:, :half] = noise[0] + mix * before[0]
        x_ref[:, half:] = noise[1] + mix * before[1]

        @pl.when(here < count - 1)
        def _():
            neighbour().wait_send()

    others(lambda i, c: inside(i, c).wait_send())

    @pl.loop(group + 1, outer)
    def _(g):
        onward(g, 0).wait_send()
        onward(g, 1).wait_send()


def run_attention(x, patch, tables, mods, q_w, kv_w, out_w, rows_own):
    width = q_w.shape[0]
    seq = x.shape[1]
    tile = 256
    flops = 2 * seq * width * 2 * width + 4 * rows_own * width * width + 16 * rows_own * seq * width
    return pl.pallas_call(
        functools.partial(attention_kernel, tile),
        out_shape=jax.ShapeDtypeStruct((rows_own, width), F32),
        in_specs=[VM] * 7 + [ANY] * 3,
        out_specs=VM,
        scratch_shapes=[
            pltpu.VMEM((seq, 2 * width), BF16),
            pltpu.VMEM((rows_own, width), BF16),
            pltpu.VMEM((rows_own, width), BF16),
            pltpu.VMEM(q_w.shape, BF16),
            pltpu.VMEM(kv_w.shape, BF16),
            pltpu.VMEM(out_w.shape, BF16),
            pltpu.SemaphoreType.DMA((3,)),
        ],
        compiler_params=pltpu.CompilerParams(vmem_limit_bytes=LIMIT),
        cost_estimate=pl.CostEstimate(
            flops=flops, bytes_accessed=8_000_000, transcendentals=rows_own * seq * width // 64
        ),
        name="attention",
    )(x, patch, *tables, mods, q_w, kv_w, out_w)


def run_mlp(coefs, x_own, h, mods, final_t, up_a, up_b, down_a, down_b):
    rows_own, width = h.shape
    units = up_a.shape[1]
    return pl.pallas_call(
        functools.partial(mlp_kernel, 256, 512),
        out_shape=jax.ShapeDtypeStruct((final_t.shape[0], rows_own), BF16),
        in_specs=[VM] * 5 + [ANY] * 4,
        out_specs=VM,
        scratch_shapes=[
            pltpu.VMEM((rows_own, width), BF16),
            pltpu.VMEM((rows_own, width), F32),
            pltpu.VMEM((2, width, units), BF16),
            pltpu.VMEM((2, units, width), BF16),
            pltpu.SemaphoreType.DMA((4,)),
        ],
        compiler_params=pltpu.CompilerParams(vmem_limit_bytes=LIMIT),
        cost_estimate=pl.CostEstimate(
            flops=8 * rows_own * width * units, bytes_accessed=12_000_000, transcendentals=0
        ),
        name="feed_forward",
    )(coefs, x_own, h, mods, final_t, up_a, up_b, down_a, down_b)


def run_prefix(count, drift, noise, mix, sums=None):
    part = drift.shape
    inner = 1
    while inner * inner < count:
        inner *= 2
    last = sums is not None
    both = jax.ShapeDtypeStruct((2,) + part, F32)
    flat = jax.ShapeDtypeStruct((part[0], 2 * part[1]), F32)
    small = jax.ShapeDtypeStruct((8, 128), F32)
    return pl.pallas_call(
        functools.partial(prefix_kernel, count, inner, last),
        out_shape=(flat, small) if last else (both, flat, small),
        in_specs=[VM] * (4 if last else 3),
        out_specs=(VM,) * (2 if last else 3),
        scratch_shapes=[
            pltpu.VMEM((inner, 2) + part, BF16),
            pltpu.VMEM((count // inner, 2) + part, BF16),
            pltpu.VMEM(part, BF16),
            pltpu.VMEM((8, 128), F32),
            pltpu.SemaphoreType.DMA((inner, 2)),
            pltpu.SemaphoreType.DMA((inner, 2)),
            pltpu.SemaphoreType.DMA((count // inner, 2)),
            pltpu.SemaphoreType.DMA((count // inner, 2)),
            pltpu.SemaphoreType.DMA((1,)),
            pltpu.SemaphoreType.DMA((1,)),
        ],
        compiler_params=pltpu.CompilerParams(
            collective_id=1 if last else 0, has_side_effects=True
        ),
        name="prefix_last" if last else "prefix",
    )(drift, noise, mix, *((sums,) if last else ()))


def run_setup(times, label, noise, mixing, table, time_in, time_out, ada, final_ada):
    patch, seq = noise.shape
    width = time_out.shape[0]
    small = jax.ShapeDtypeStruct((8, 128), F32)
    return pl.pallas_call(
        setup_kernel,
        out_shape=(
            jax.ShapeDtypeStruct((8, width), F32),
            small,
            small,
            jax.ShapeDtypeStruct((2, patch, seq // 2), F32),
            jax.ShapeDtypeStruct((patch, seq), F32),
        ),
        in_specs=[SM, SM, VM, VM] + [ANY] * 5,
        out_specs=(VM,) * 5,
        scratch_shapes=[
            pltpu.VMEM((8, width), BF16),
            pltpu.VMEM(time_in.shape, BF16),
            pltpu.VMEM(time_out.shape, BF16),
            pltpu.VMEM(ada.shape, BF16),
            pltpu.VMEM(final_ada.shape, BF16),
            pltpu.SemaphoreType.DMA((11,)),
        ],
        compiler_params=pltpu.CompilerParams(vmem_limit_bytes=LIMIT),
        cost_estimate=pl.CostEstimate(flops=0, bytes_accessed=12_000_000, transcendentals=0),
        name="setup",
    )(times, label, noise, mixing, table, time_in, time_out, ada, final_ada)


def per_device(
    noise_start,
    timesteps,
    class_labels,
    mixing,
    class_table,
    time_in,
    time_out,
    ada_weight,
    final_ada,
    patch_weight,
    q_weight,
    kv_weight,
    out_weight,
    up_weight,
    down_weight,
    final_weight,
):
    count = lax.axis_size("tm")
    patch, width = patch_weight.shape
    seq = noise_start.shape[1] // patch
    rows_own = seq // 2
    swap = [(0, 1), (1, 0)]
    up_other = lax.ppermute(up_weight, "tensor", swap)
    down_other = lax.ppermute(down_weight, "tensor", swap)

    plain = noise_start.reshape(seq, patch).T
    mods, coefs, mix, noise, x = run_setup(
        timesteps, class_labels, plain, mixing, class_table, time_in, time_out, ada_weight, final_ada
    )

    half_width = width // 2
    rates = np.exp(-math.log(10000.0) * np.arange(half_width) / half_width)
    near = np.arange(PERIOD)[:, None] * rates[None]
    far = np.arange(seq // PERIOD)[:, None] * PERIOD * rates[None]
    tables = [
        jnp.asarray(t.astype(np.float32))
        for t in (np.sin(far), np.cos(far), np.sin(near), np.cos(near))
    ]
    final_t = final_weight.T

    def drift_of(x):
        h = run_attention(
            x, patch_weight, tables, mods, q_weight, kv_weight, out_weight, rows_own
        )
        return run_mlp(coefs, x, h, mods, final_t, up_weight, up_other, down_weight, down_other)

    sums, x, first = run_prefix(count, drift_of(x), noise, mix)
    state, second = run_prefix(count, drift_of(x), noise, mix, sums)
    states = state.T.reshape(1, 1, seq * patch)
    return (states, jnp.stack([first[0, 0], second[0, 0]])[:, None])


def solution(mesh):
    in_specs = (
        P(),
        P(),
        P("tm", None),
        P(None, "tm"),
        P(),
        P(),
        P(),
        P(),
        P(),
        P(),
        P(),
        P(),
        P(),
        P(None, "tensor"),
        P("tensor", None),
        P(),
    )
    out_specs = (P("tm", None, None), P(None, "tm"))
    return jax.shard_map(
        per_device, mesh=mesh, in_specs=in_specs, out_specs=out_specs, check_vma=False
    )
```

time: 135 us -> 117 us (0.87); the launches traced: 132 us -> 117 us
  matrix products: 7.19 us -> 0 us
  between operations: 7.98 us -> 1.38 us
  other arithmetic: 9.62 us -> 3.48 us
  Pallas kernels: 97.5 us -> 103 us
  starting transfers between devices: 5.57 us -> 0.64 us
  local copies, waits for them, and re-layouts: 4.63 us -> 8.55 us
    pallas_call x2 -> x3, Pallas kernels: 24.3 us -> 32 us  [the longest x2 25.9 us: run_prefix(): pl.pallas_call(functools.partial(prefix_kernel, count, inner, last), out_...]
    dot_general x4 -> x0, matrix products: 7.19 us -> none  [the longest x1 4.02 us: per_device(): modul = jnp.dot(cond, ada_weight, preferred_element_type=F32)]
    ppermute x1 -> x0, starting transfers between devices: 4.93 us -> none  [per_device(): lax.ppermute(mixing, 'tm', [(i, i + 1) for i in range(count - 1)])]
    reduce_sum x3 -> x0, other arithmetic: 3.59 us -> none  [the longest x1 2.1 us: per_device(): residuals = [jnp.mean(jnp.square(sums))]]
    unnamed x14 -> x4, local copies, waits for them, and re-layouts: 0.56 us -> 3.21 us
    pallas_call x2, Pallas kernels: 26.8 us -> 24.2 us  [run_mlp(): pl.pallas_call(functools.partial(mlp_kernel, 256, 512), out_shape=jax.Sha...]
    another operation x3 -> x0, other arithmetic: 1.99 us -> none  [the longest x1 1.37 us: per_device(): jnp.stack([pick_entry(timesteps, point), pick_entry(timesteps, point + 1)])]
  transfers between devices with their start and end apart: 3 -> 2, of which waited for: 0 -> 0; matrix products, arithmetic and copies ran while one was open for 12% -> 4% of each run, Pallas kernels for 17% -> 25%
where the time goes in v2:
time: 117 us
  Pallas kernels  103 us (88%)
  local copies, waits for them, and re-layouts  8.55 us (7%)
  other arithmetic  3.48 us (3%)
  between operations  1.38 us (1%)
    pallas_call x2, Pallas kernels, run_attention(): pl.pallas_call(functools.partial(attention_kernel, tile), out_shape=jax.S...  46.3 us
    pallas_call x2, Pallas kernels, run_prefix(): pl.pallas_call(functools.partial(prefix_kernel, count, inner, last), out_...  25.9 us
    pallas_call x2, Pallas kernels, run_mlp(): pl.pallas_call(functools.partial(mlp_kernel, 256, 512), out_shape=jax.Sha...  24.2 us
    pallas_call x1, Pallas kernels, run_setup(): pl.pallas_call(setup_kernel, out_shape=(jax.ShapeDtypeStruct((8, width),...  6.1 us
    unnamed x4, local copies, waits for them, and re-layouts  3.21 us
    slice x2, local copies, waits for them, and re-layouts, per_device(): return (states, jnp.stack([first[0, 0], second[0, 0]])[:, None])  2.46 us
  transfers between devices with their start and end apart: 2, of which 0 were waited for; matrix products, arithmetic and copies ran while one was open for 4% of the time, Pallas kernels for 25%

profile of v2, /device:TPU:0, one launch (start us, length us, event | category | flops | bytes accessed | tf_op | source)
XLA Modules:
  0.0 116.6 jit_solution(3568933571326085274)
XLA Ops:
  0.6 0.6 collective-permute-start
  1.2 0.1 collective-permute-start.1
  1.9 1.3 %copy.24.mixing_ref = f32[2,1]{1,0:T(2,128)} copy(f32[2,1]{0,1:T(1,128)} %param.23) | data formatting | bytes 16 | tf_op args[3]
  3.2 0.5 broadcast.3
  3.7 1.6 %reduce.3 = f32[16384]{0:T(1024)S(1)} reduce(f32[1,16384]{1,0:T(1,128)} %param.20, f32[]{:T(128)} %broadcast.3), dimensions={0}, to_apply=%param.20.reduce_sub_computation.3 | reduce | bytes 131076 | tf_op args[0]
  5.4 0.2 reshape.10
  5.6 0.8 copy.23
  6.4 6.1 %setup.1 = (f32[8,768]{1,0:T(8,128)}, f32[8,128]{1,0:T(8,128)}, f32[8,128]{1,0:T(8,128)}, f32[2,16,512]{2,1,0:T(8,128)}, f32[16,1024]{1,0:T(8,128)}) custom-call(s32[17]{0:T(128)} %times_ref.1, s32[1,1]{1,0:T(1,128)S(6)} %copy.26.label_ref, f32[16,1024]{1,0:T(8,128)} %bitcast.7, f32[2,1]{1,0:T(2,128)} %copy.24.mixing_ref, bf16[1000,768]{1,0:T(8,128)(2,1)} %table_hbm.1, ...), custom_call_target="tpu_custom_call" | custom-call | bytes 12000000 | tf_op jit(solution)/shard_map/setup/pallas_call | solution.py:554
  12.5 23.2 %attention.2.h_ref = f32[512,768]{1,0:T(8,128)} custom-call(f32[16,1024]{1,0:T(8,128)} %get-tuple-element.13.x_ref, bf16[16,768]{1,0:T(8,128)(2,1)} %patch_ref.3, f32[32,384]{1,0:T(8,128)} %constant.8.clone.far_sin, f32[32,384]{1,0:T(8,128)} %constant.9.clone.far_cos, f32[32,384]{1,0:T(8,128)} %constant.10.clone.near_sin, ...), custom_call_target="tpu_custom_call" | custom-call | flops 10066329600 | bytes 8000000 | tf_op jit(solution)/shard_map/attention/pallas_call | solution.py:472
  35.7 0.0 collective-permute-done.up_b
  35.7 0.0 copy-start
  35.7 0.0 collective-permute-done.1.down_b
  35.7 1.4 %copy-done = bf16[768,1536]{1,0:T(8,128)(2,1)} copy-done((bf16[768,1536]{1,0:T(8,128)(2,1)}, bf16[768,1536]{1,0:T(8,128)(2,1)S(1)}, u32[]{:S(2)}) %copy-start) | copy-done | bytes 2359320
  37.1 12.1 %feed_forward.2.d_ref = bf16[16,512]{1,0:T(8,128)(2,1)} custom-call(f32[8,128]{1,0:T(8,128)} %get-tuple-element.12.coef_ref, f32[16,1024]{1,0:T(8,128)} %get-tuple-element.13.x_ref, f32[512,768]{1,0:T(8,128)} %attention.2.h_ref, f32[8,768]{1,0:T(8,128)} %get-tuple-element.14.mod_ref, bf16[16,768]{1,0:T(8,128)(2,1)} %bitcast.9, bf16[768,1536]{1,0:T(8,128)(2,1)} %up_a.3, ...), custom_call_target="tpu_custom_call" | custom-call | flops 4831838208 | bytes 12000000 | tf_op jit(solution)/shard_map/feed_forward/pallas_call | solution.py:497
  49.2 13.7 %prefix.1 = (f32[2,16,512]{2,1,0:T(8,128)}, f32[16,1024]{1,0:T(8,128)}, f32[8,128]{1,0:T(8,128)}) custom-call(bf16[16,512]{1,0:T(8,128)(2,1)} %feed_forward.2.d_ref, f32[2,16,512]{2,1,0:T(8,128)} %get-tuple-element.15.noise_ref, f32[8,128]{1,0:T(8,128)} %get-tuple-element.16.mix_ref), custom_call_target="tpu_custom_call" | custom-call | tf_op jit(solution)/shard_map/prefix/pallas_call | solution.py:526
  63.0 1.2 %slice.6 = f32[1,1]{1,0:T(1,128)} slice(f32[8,128]{1,0:T(8,128)} %get-tuple-element.20), slice={[0:1], [0:1]} | slice | bytes 8 | tf_op jit(solution)/shard_map/slice | solution.py:629
  64.2 23.2 %attention.3.h_ref = f32[512,768]{1,0:T(8,128)} custom-call(f32[16,1024]{1,0:T(8,128)} %get-tuple-element.17.x_ref, bf16[16,768]{1,0:T(8,128)(2,1)} %patch_ref.3, f32[32,384]{1,0:T(8,128)} %constant.8.clone.far_sin, f32[32,384]{1,0:T(8,128)} %constant.9.clone.far_cos, f32[32,384]{1,0:T(8,128)} %constant.10.clone.near_sin, ...), custom_call_target="tpu_custom_call" | custom-call | flops 10066329600 | bytes 8000000 | tf_op jit(solution)/shard_map/attention/pallas_call | solution.py:472
  87.3 12.1 %feed_forward.3.d_ref = bf16[16,512]{1,0:T(8,128)(2,1)} custom-call(f32[8,128]{1,0:T(8,128)} %get-tuple-element.12.coef_ref, f32[16,1024]{1,0:T(8,128)} %get-tuple-element.17.x_ref, f32[512,768]{1,0:T(8,128)} %attention.3.h_ref, f32[8,768]{1,0:T(8,128)} %get-tuple-element.14.mod_ref, bf16[16,768]{1,0:T(8,128)(2,1)} %bitcast.10, bf16[768,1536]{1,0:T(8,128)(2,1)} %up_a.3, ...), custom_call_target="tpu_custom_call" | custom-call | flops 4831838208 | bytes 12000000 | tf_op jit(solution)/shard_map/feed_forward/pallas_call | solution.py:497
  99.5 12.1 %prefix_last.1 = (f32[16,1024]{1,0:T(8,128)}, f32[8,128]{1,0:T(8,128)}) custom-call(bf16[16,512]{1,0:T(8,128)(2,1)} %feed_forward.3.d_ref, f32[2,16,512]{2,1,0:T(8,128)} %get-tuple-element.15.noise_ref, f32[8,128]{1,0:T(8,128)} %get-tuple-element.16.mix_ref, f32[2,16,512]{2,1,0:T(8,128)} %get-tuple-element.18.rest_0_), custom_call_target="tpu_custom_call" | custom-call | tf_op jit(solution)/shard_map/prefix_last/pallas_call | solution.py:526
  111.6 1.3 %slice.7 = f32[1,1]{1,0:T(1,128)} slice(f32[8,128]{1,0:T(8,128)} %get-tuple-element.21), slice={[0:1], [0:1]} | slice | bytes 8 | tf_op jit(solution)/shard_map/slice | solution.py:629
  112.9 1.0 copy.25
  113.9 0.9 reshape.11
  114.8 1.8 %maximum_bitcast_fusion = f32[2,1]{0,1:T(1,128)} fusion(f32[1]{0:T(128)} %bitcast.4, f32[1]{0:T(128)} %bitcast.3), kind=kLoop, calls=%fused_computation | loop fusion | flops 2 | bytes 16 | tf_op jit(solution)/shard_map/broadcast_in_dim | solution.py:629
Async XLA Ops:
  0.6 35.0 %collective-permute-start = (bf16[768,1536]{1,0:T(8,128)(2,1)}, bf16[768,1536]{1,0:T(8,128)(2,1)S(1)}, u32[]{:S(2)}, u32[]{:S(2)}) collective-permute-start(bf16[768,1536]{1,0:T(8,128)(2,1)} %up_a.3), channel_id=1, source_target_pairs={{0,1},{1,0},{2,3},{3,2},{4,5},{5,4},{6,7},{7,6},{8,9},{9,8},{10,11... | collective-permute-start | bytes 7077896 | tf_op jit(solution)/shard_map/ppermute | solution.py:602
  1.2 34.5 %collective-permute-start.1 = (bf16[1536,768]{1,0:T(8,128)(2,1)}, bf16[1536,768]{1,0:T(8,128)(2,1)}, u32[]{:S(2)}, u32[]{:S(2)}) collective-permute-start(bf16[1536,768]{1,0:T(8,128)(2,1)} %down_a.3), channel_id=1, source_target_pairs={{0,1},{1,0},{2,3},{3,2},{4,5},{5,4},{6,7},{7,6},{8,9},{9,8},{10,11... | collective-permute-start | bytes 7077896 | tf_op jit(solution)/shard_map/ppermute | solution.py:603
  35.7 1.4 %copy-start = (bf16[768,1536]{1,0:T(8,128)(2,1)}, bf16[768,1536]{1,0:T(8,128)(2,1)S(1)}, u32[]{:S(2)}) copy-start(bf16[768,1536]{1,0:T(8,128)(2,1)S(1)} %collective-permute-done.up_b) | copy-start | bytes 7077892

commit v3 on v2

--- a/solution.py
+++ b/solution.py
@@ -11,7 +11,7 @@
 
 HEAD_DIM = 64
 ITERS = 2
-PERIOD = 32
+LANES = 128
 norm_eps = 1e-06
 plan_steps = 1000
 MESH = pl.DeviceIdType.MESH
@@ -42,9 +42,11 @@
     kv_hbm,
     out_hbm,
     h_ref,
+    in_s,
     kv_s,
     q_s,
     att_s,
+    value_s,
     q_w,
     kv_w,
     out_w,
@@ -59,49 +61,55 @@
     for copy in copies:
         copy.start()
     shift, scale, gate = mod_ref[0:1, :], 1.0 + mod_ref[1:2, :], mod_ref[2:3, :]
-    groups = tile // PERIOD
-    spans = far_sin.shape[0]
+    lines = far_sin.shape[0]
+    spans = seq // lines
     member = lax.axis_index("tensor")
+    fs, fc = far_sin[...], far_cos[...]
 
     def embed(t):
-        rows = pl.ds(pl.multiple_of(t * tile, tile), tile)
-        tokens = x_ref[:, rows].astype(BF16)
+        rows = slice(t * tile, (t + 1) * tile)
         hidden = lax.dot_general(
-            tokens, patch_ref[...], (((0,), (0,)), ((), ())), preferred_element_type=F32
+            x_ref[:, rows].astype(BF16),
+            patch_ref[...],
+            (((0,), (0,)), ((), ())),
+            preferred_element_type=F32,
         )
-        turn = lax.rem(t * groups + member * (spans // 2), spans)
-        far = pl.ds(pl.multiple_of(turn, groups), groups)
-        fs, fc = far_sin[far, :][:, None, :], far_cos[far, :][:, None, :]
-        ns, nc = near_sin[...][None], near_cos[...][None]
-        sines = (fs * nc + fc * ns).reshape(tile, width // 2)
-        cosines = (fc * nc - fs * ns).reshape(tile, width // 2)
-        hidden = hidden + jnp.concatenate([sines, cosines], axis=1)
-        return rows, hidden, (normed(hidden) * scale + shift).astype(BF16)
-
+        blocks = []
+        for i in range(tile // lines):
+            turn = lax.rem(t * (tile // lines) + i + member * (spans // 2), spans)
+            ns, nc = near_sin[pl.ds(turn, 1), :], near_cos[pl.ds(turn, 1), :]
+            blocks.append(jnp.concatenate([fs * nc + fc * ns, fc * nc - fs * ns], axis=1))
+        hidden = hidden + jnp.concatenate(blocks, axis=0)
+        if t * tile < rows_own:
+            h_ref[rows, :] = hidden
+        in_s[rows, :] = (normed(hidden) * scale + shift).astype(BF16)
+
+    def project(t):
+        rows = slice(t * tile, (t + 1) * tile)
+        attn_in = in_s[rows, :]
+        kv_s[rows, :] = jnp.dot(attn_in, kv_w[...], preferred_element_type=F32).astype(BF16)
+        if t * tile < rows_own:
+            q = jnp.dot(attn_in, q_w[...], preferred_element_type=F32).astype(BF16)
+            q_s[rows, :] = q * BF16(1.0 / math.sqrt(HEAD_DIM))
+
+    pair = 2 * HEAD_DIM
+    value_s[:, pair:] = jnp.ones((seq, pair), BF16)
+    embed(0)
     copies[0].wait()
     copies[1].wait()
-
-    @pl.loop(0, rows_own // tile)
-    def _(t):
-        rows, hidden, attn_in = embed(t)
-        h_ref[rows, :] = hidden
-        kv_s[rows, :] = jnp.dot(attn_in, kv_w[...], preferred_element_type=F32).astype(BF16)
-        q = jnp.dot(attn_in, q_w[...], preferred_element_type=F32).astype(BF16)
-        q_s[rows, :] = q * BF16(1.0 / math.sqrt(HEAD_DIM))
-
-    @pl.loop(rows_own // tile, seq // tile)
-    def _(t):
-        rows, _, attn_in = embed(t)
-        kv_s[rows, :] = jnp.dot(attn_in, kv_w[...], preferred_element_type=F32).astype(BF16)
-
-    pair = 2 * HEAD_DIM
+    for t in range(seq // tile):
+        if (t + 1) * tile < seq:
+            embed(t + 1)
+        project(t)
+
     first = lax.broadcasted_iota(jnp.int32, (tile, pair), 1) < HEAD_DIM
 
     @pl.loop(0, width // pair)
     def _(hp):
         cols = pl.ds(pl.multiple_of(hp * pair, pair), pair)
         keys = kv_s[:, cols]
-        values = kv_s[:, pl.ds(pl.multiple_of(width + hp * pair, pair), pair)]
+        value_s[:, :pair] = kv_s[:, pl.ds(pl.multiple_of(width + hp * pair, pair), pair)]
+        values = value_s[...]
         for t in range(rows_own // tile):
             rows = slice(t * tile, (t + 1) * tile)
             q2 = q_s[rows, cols]
@@ -113,10 +121,9 @@
                     (((1,), (1,)), ((), ())),
                     preferred_element_type=F32,
                 )
-                p = jnp.exp(s - jnp.max(s, axis=-1, keepdims=True))
-                total = jnp.sum(p, axis=-1, keepdims=True)
-                o = jnp.dot(p.astype(BF16), values, preferred_element_type=F32)
-                outs.append(o * (1.0 / total))
+                p = jnp.exp(s - jnp.max(s, axis=-1, keepdims=True)).astype(BF16)
+                o = jnp.dot(p, values, preferred_element_type=F32)
+                outs.append(o[:, :pair] / o[:, pair:])
             att_s[rows, cols] = jnp.where(first, outs[0], outs[1]).astype(BF16)
 
     copies[2].wait()
@@ -254,12 +261,17 @@
     coef_ref[0:1, :] = jnp.broadcast_to(keep, (1, 128))
     coef_ref[1:2, :] = jnp.broadcast_to(noise, (1, 128))
     coef_ref[2:8, :] = jnp.zeros((6, 128), F32)
-    mix_ref[0:2, :] = jnp.broadcast_to(mixing_ref[...], (2, 128))
+    mix_ref[0:1, :] = jnp.full((1, 128), mixing_ref[0, 0], F32)
+    mix_ref[1:2, :] = jnp.full((1, 128), mixing_ref[0, 1], F32)
     mix_ref[2:8, :] = jnp.zeros((6, 128), F32)
 
-    plain = noise_ref[...]
-    half = plain.shape[1] // 2
-    left, right = plain[:, :half], plain[:, half:]
+    turned = noise_ref[...].T
+    patch = x_ref.shape[0]
+    blocks = turned.shape[0] // patch // 2
+    low = [turned[i * patch : (i + 1) * patch] for i in range(blocks)]
+    high = [turned[(blocks + i) * patch : (blocks + i + 1) * patch] for i in range(blocks)]
+    left, right = jnp.concatenate(low, axis=1), jnp.concatenate(high, axis=1)
+    half = left.shape[1]
     first = member == 0
     own, other = jnp.where(first, left, right), jnp.where(first, right, left)
     halves_ref[0] = own
@@ -294,7 +306,7 @@
     *rest,
 ):
     if last:
-        sums_in, state_ref, res_ref, *rest = rest
+        sums_in, res_in, state_ref, res_ref, *rest = rest
     else:
         sums_out, x_ref, res_ref, *rest = rest
     held, totals, mine, mix_in, send_a, recv_a, send_b, recv_b, send_m, recv_m = rest
@@ -426,23 +438,25 @@
     def mean_square(values):
         total = sum(v * v for v in values)
         total = jnp.sum(jnp.sum(total, axis=1, keepdims=True), axis=0, keepdims=True)
-        return jnp.broadcast_to(total * scale, res_ref.shape)
+        return total * scale
 
     mix = mix_ref[0:1, 0:1]
     if last:
         old = [sums_in[0], sums_in[1]]
         state = [n + (1.0 + mix) * o for n, o in zip(noise, old)]
         picard = [n + s for n, s in zip(noise, sums)]
-        res_ref[...] = mean_square([g - s for g, s in zip(picard, state)])
+        second = mean_square([g - s for g, s in zip(picard, state)])
+        res_ref[...] = jnp.concatenate([res_in[0:1, 0:1], second], axis=1)
         mix = mix_ref[1:2, 0:1]
         new = [g + mix * (s - o) for g, s, o in zip(picard, sums, old)]
         first = core == 0
-        state_ref[:, :half] = jnp.where(first, new[0], new[1])
-        state_ref[:, half:] = jnp.where(first, new[1], new[0])
+        low, high = jnp.where(first, new[0], new[1]), jnp.where(first, new[1], new[0])
+        blocks = [v[:, i : i + LANES] for v in (low, high) for i in range(0, half, LANES)]
+        state_ref[...] = jnp.concatenate(blocks, axis=0).T
     else:
         sums_out[0] = sums[0]
         sums_out[1] = sums[1]
-        res_ref[...] = mean_square(sums)
+        res_ref[...] = jnp.broadcast_to(mean_square(sums), res_ref.shape)
 
         @pl.when(here > 0)
         def _():
@@ -475,9 +489,11 @@
         in_specs=[VM] * 7 + [ANY] * 3,
         out_specs=VM,
         scratch_shapes=[
+            pltpu.VMEM((seq, width), BF16),
             pltpu.VMEM((seq, 2 * width), BF16),
             pltpu.VMEM((rows_own, width), BF16),
             pltpu.VMEM((rows_own, width), BF16),
+            pltpu.VMEM((seq, 4 * HEAD_DIM), BF16),
             pltpu.VMEM(q_w.shape, BF16),
             pltpu.VMEM(kv_w.shape, BF16),
             pltpu.VMEM(out_w.shape, BF16),
@@ -514,19 +530,21 @@
     )(coefs, x_own, h, mods, final_t, up_a, up_b, down_a, down_b)
 
 
-def run_prefix(count, drift, noise, mix, sums=None):
+def run_prefix(count, drift, noise, mix, *carried):
     part = drift.shape
     inner = 1
     while inner * inner < count:
         inner *= 2
-    last = sums is not None
+    last = bool(carried)
     both = jax.ShapeDtypeStruct((2,) + part, F32)
     flat = jax.ShapeDtypeStruct((part[0], 2 * part[1]), F32)
+    square = jax.ShapeDtypeStruct((2 * part[0] * part[1] // LANES, LANES), F32)
+    ends = jax.ShapeDtypeStruct((1, 2), F32)
     small = jax.ShapeDtypeStruct((8, 128), F32)
     return pl.pallas_call(
         functools.partial(prefix_kernel, count, inner, last),
-        out_shape=(flat, small) if last else (both, flat, small),
-        in_specs=[VM] * (4 if last else 3),
+        out_shape=(square, ends) if last else (both, flat, small),
+        in_specs=[VM] * (5 if last else 3),
         out_specs=(VM,) * (2 if last else 3),
         scratch_shapes=[
             pltpu.VMEM((inner, 2) + part, BF16),
@@ -544,11 +562,11 @@
             collective_id=1 if last else 0, has_side_effects=True
         ),
         name="prefix_last" if last else "prefix",
-    )(drift, noise, mix, *((sums,) if last else ()))
-
-
-def run_setup(times, label, noise, mixing, table, time_in, time_out, ada, final_ada):
-    patch, seq = noise.shape
+    )(drift, noise, mix, *carried)
+
+
+def run_setup(patch, times, label, noise, mixing, table, time_in, time_out, ada, final_ada):
+    seq = noise.size // patch
     width = time_out.shape[0]
     small = jax.ShapeDtypeStruct((8, 128), F32)
     return pl.pallas_call(
@@ -560,7 +578,7 @@
             jax.ShapeDtypeStruct((2, patch, seq // 2), F32),
             jax.ShapeDtypeStruct((patch, seq), F32),
         ),
-        in_specs=[SM, SM, VM, VM] + [ANY] * 5,
+        in_specs=[SM, SM, VM, SM] + [ANY] * 5,
         out_specs=(VM,) * 5,
         scratch_shapes=[
             pltpu.VMEM((8, width), BF16),
@@ -602,15 +620,24 @@
     up_other = lax.ppermute(up_weight, "tensor", swap)
     down_other = lax.ppermute(down_weight, "tensor", swap)
 
-    plain = noise_start.reshape(seq, patch).T
     mods, coefs, mix, noise, x = run_setup(
-        timesteps, class_labels, plain, mixing, class_table, time_in, time_out, ada_weight, final_ada
+        patch,
+        timesteps,
+        class_labels,
+        noise_start.reshape(noise_start.size // LANES, LANES),
+        mixing.T,
+        class_table,
+        time_in,
+        time_out,
+        ada_weight,
+        final_ada,
     )
 
     half_width = width // 2
-    rates = np.exp(-math.log(10000.0) * np.arange(half_width) / half_width)
-    near = np.arange(PERIOD)[:, None] * rates[None]
-    far = np.arange(seq // PERIOD)[:, None] * PERIOD * rates[None]
+    rates = np.exp(-math.log(10000.0) * np.arange(half_width) / half_width)[None]
+    spans = LANES // patch
+    far = spans * np.arange(seq // spans)[:, None] * rates
+    near = np.arange(spans)[:, None] * rates
     tables = [
         jnp.asarray(t.astype(np.float32))
         for t in (np.sin(far), np.cos(far), np.sin(near), np.cos(near))
@@ -624,9 +651,8 @@
         return run_mlp(coefs, x, h, mods, final_t, up_weight, up_other, down_weight, down_other)
 
     sums, x, first = run_prefix(count, drift_of(x), noise, mix)
-    state, second = run_prefix(count, drift_of(x), noise, mix, sums)
-    states = state.T.reshape(1, 1, seq * patch)
-    return (states, jnp.stack([first[0, 0], second[0, 0]])[:, None])
+    state, residuals = run_prefix(count, drift_of(x), noise, mix, sums, first)
+    return (state.reshape((1,) + noise_start.shape), residuals.T)
 
 
 def solution(mesh):

time: 117 us -> 102 us (0.87)
  Pallas kernels: 103 us -> 95.2 us
  local copies, waits for them, and re-layouts: 8.55 us -> 4.7 us
  other arithmetic: 3.48 us -> 0 us
    pallas_call x2, Pallas kernels: 46.3 us -> 39 us  [run_attention(): pl.pallas_call(functools.partial(attention_kernel, tile), out_shape=jax.S...]
    slice x2 -> x0, local copies, waits for them, and re-layouts: 2.46 us -> none  [per_device(): return (states, jnp.stack([first[0, 0], second[0, 0]])[:, None])]
    reshape x3 -> x0, local copies, waits for them, and re-layouts: 1.85 us -> none  [the longest x2 0.98 us: per_device(): plain = noise_start.reshape(seq, patch).T]
    broadcast_in_dim x1 -> x0, other arithmetic: 1.84 us -> none  [per_device(): return (states, jnp.stack([first[0, 0], second[0, 0]])[:, None])]
    unnamed x1 -> x0, other arithmetic: 1.64 us -> none
    unnamed x4 -> x6, local copies, waits for them, and re-layouts: 3.21 us -> 4.7 us
  transfers between devices with their start and end apart: 2 -> 2, of which waited for: 0 -> 0; matrix products, arithmetic and copies ran while one was open for 4% -> 0% of each run, Pallas kernels for 25% -> 25%
where the time goes in v3:
time: 102 us
  Pallas kernels  95.2 us (93%)
  local copies, waits for them, and re-layouts  4.7 us (5%)
  between operations  1.37 us (1%)
    pallas_call x2, Pallas kernels, run_attention(): pl.pallas_call(functools.partial(attention_kernel, tile), out_shape=jax.S...  39 us
    pallas_call x2, Pallas kernels, run_prefix(): pl.pallas_call(functools.partial(prefix_kernel, count, inner, last), out_...  25.9 us
    pallas_call x2, Pallas kernels, run_mlp(): pl.pallas_call(functools.partial(mlp_kernel, 256, 512), out_shape=jax.Sha...  24.2 us
    pallas_call x1, Pallas kernels, run_setup(): pl.pallas_call(setup_kernel, out_shape=(jax.ShapeDtypeStruct((8, width),...  6.11 us
    unnamed x6, local copies, waits for them, and re-layouts  4.7 us
  transfers between devices with their start and end apart: 2, of which 0 were waited for; matrix products, arithmetic and copies ran while one was open for 0% of the time, Pallas kernels for 25%

profile of v3, /device:TPU:0, one launch (start us, length us, event | category | flops | bytes accessed | tf_op | source)
XLA Modules:
  0.0 102.0 jit_solution(11795057870222595827)
XLA Ops:
  0.6 0.6 collective-permute-start
  1.2 0.1 collective-permute-start.1
  1.9 6.1 %setup.1 = (f32[8,768]{1,0:T(8,128)}, f32[8,128]{1,0:T(8,128)}, f32[8,128]{1,0:T(8,128)}, f32[2,16,512]{2,1,0:T(8,128)}, f32[16,1024]{1,0:T(8,128)}) custom-call(s32[17]{0:T(128)} %times_ref.1, s32[1,1]{1,0:T(1,128)S(6)} %copy.24.label_ref, f32[128,128]{1,0:T(8,128)} %bitcast.5, f32[1,2]{1,0:T(1,128)} %bitcast.7, bf16[1000,768]{1,0:T(8,128)(2,1)} %table_hbm.1, ...), custom_call_target="tpu_custom_call" | custom-call | bytes 12000000 | tf_op jit(solution)/shard_map/setup/pallas_call | solution.py:572
  8.0 19.5 %attention.2.h_ref = f32[512,768]{1,0:T(8,128)} custom-call(f32[16,1024]{1,0:T(8,128)} %get-tuple-element.13.x_ref, bf16[16,768]{1,0:T(8,128)(2,1)} %patch_ref.3, f32[128,384]{1,0:T(8,128)} %constant.8.clone.far_sin, f32[128,384]{1,0:T(8,128)} %constant.9.clone.far_cos, f32[8,384]{1,0:T(8,128)} %constant.10.clone.near_sin, ...), custom_call_target="tpu_custom_call" | custom-call | flops 10066329600 | bytes 8000000 | tf_op jit(solution)/shard_map/attention/pallas_call | solution.py:486
  27.6 0.0 collective-permute-done.up_b
  27.6 0.0 copy-start
  27.6 0.0 collective-permute-done.1.down_b
  27.6 0.0 copy-start.1
  27.6 1.4 %copy-done = bf16[768,1536]{1,0:T(8,128)(2,1)} copy-done((bf16[768,1536]{1,0:T(8,128)(2,1)}, bf16[768,1536]{1,0:T(8,128)(2,1)S(1)}, u32[]{:S(2)}) %copy-start) | copy-done | bytes 2359320
  29.0 0.7 copy-done.1
  29.7 12.1 %feed_forward.2.d_ref = bf16[16,512]{1,0:T(8,128)(2,1)} custom-call(f32[8,128]{1,0:T(8,128)} %get-tuple-element.12.coef_ref, f32[16,1024]{1,0:T(8,128)} %get-tuple-element.13.x_ref, f32[512,768]{1,0:T(8,128)} %attention.2.h_ref, f32[8,768]{1,0:T(8,128)} %get-tuple-element.14.mod_ref, bf16[16,768]{1,0:T(8,128)(2,1)} %bitcast.8, bf16[768,1536]{1,0:T(8,128)(2,1)} %up_a.3, ...), custom_call_target="tpu_custom_call" | custom-call | flops 4831838208 | bytes 12000000 | tf_op jit(solution)/shard_map/feed_forward/pallas_call | solution.py:513
  41.8 13.8 %prefix.1 = (f32[2,16,512]{2,1,0:T(8,128)}, f32[16,1024]{1,0:T(8,128)}, f32[8,128]{1,0:T(8,128)}) custom-call(bf16[16,512]{1,0:T(8,128)(2,1)} %feed_forward.2.d_ref, f32[2,16,512]{2,1,0:T(8,128)} %get-tuple-element.15.noise_ref, f32[8,128]{1,0:T(8,128)} %get-tuple-element.16.mix_ref), custom_call_target="tpu_custom_call" | custom-call | tf_op jit(solution)/shard_map/prefix/pallas_call | solution.py:544
  55.6 19.5 %attention.3.h_ref = f32[512,768]{1,0:T(8,128)} custom-call(f32[16,1024]{1,0:T(8,128)} %get-tuple-element.17.x_ref, bf16[16,768]{1,0:T(8,128)(2,1)} %patch_ref.3, f32[128,384]{1,0:T(8,128)} %constant.8.clone.far_sin, f32[128,384]{1,0:T(8,128)} %constant.9.clone.far_cos, f32[8,384]{1,0:T(8,128)} %constant.10.clone.near_sin, ...), custom_call_target="tpu_custom_call" | custom-call | flops 10066329600 | bytes 8000000 | tf_op jit(solution)/shard_map/attention/pallas_call | solution.py:486
  75.1 12.1 %feed_forward.3.d_ref = bf16[16,512]{1,0:T(8,128)(2,1)} custom-call(f32[8,128]{1,0:T(8,128)} %get-tuple-element.12.coef_ref, f32[16,1024]{1,0:T(8,128)} %get-tuple-element.17.x_ref, f32[512,768]{1,0:T(8,128)} %attention.3.h_ref, f32[8,768]{1,0:T(8,128)} %get-tuple-element.14.mod_ref, bf16[16,768]{1,0:T(8,128)(2,1)} %bitcast.9, bf16[768,1536]{1,0:T(8,128)(2,1)} %up_a.3, ...), custom_call_target="tpu_custom_call" | custom-call | flops 4831838208 | bytes 12000000 | tf_op jit(solution)/shard_map/feed_forward/pallas_call | solution.py:513
  87.2 12.1 %prefix_last.1 = (f32[128,128]{1,0:T(8,128)}, f32[1,2]{1,0:T(1,128)}) custom-call(bf16[16,512]{1,0:T(8,128)(2,1)} %feed_forward.3.d_ref, f32[2,16,512]{2,1,0:T(8,128)} %get-tuple-element.15.noise_ref, f32[8,128]{1,0:T(8,128)} %get-tuple-element.16.mix_ref, f32[2,16,512]{2,1,0:T(8,128)} %get-tuple-element.18.rest_0_, f32[8,128]{1,0:T(8,128)} %get-tuple-element.19.rest_1_), custom_call_target="tpu_custom_call" | custom-call | tf_op jit(solution)/shard_map/prefix_last/pallas_call | solution.py:544
  99.4 1.5 %copy.25 = f32[1,1,16384]{2,1,0:T(1,128)} copy(f32[1,1,16384]{2,1,0:T(1,128)} %bitcast.6) | data formatting | bytes 131072
  100.8 1.1 %copy.26 = f32[2,1]{0,1:T(1,128)} copy(f32[2,1]{0,1:T(1,128)} %bitcast.10) | data formatting | bytes 16
Async XLA Ops:
  0.6 26.9 %collective-permute-start = (bf16[768,1536]{1,0:T(8,128)(2,1)}, bf16[768,1536]{1,0:T(8,128)(2,1)S(1)}, u32[]{:S(2)}, u32[]{:S(2)}) collective-permute-start(bf16[768,1536]{1,0:T(8,128)(2,1)} %up_a.3), channel_id=1, source_target_pairs={{0,1},{1,0},{2,3},{3,2},{4,5},{5,4},{6,7},{7,6},{8,9},{9,8},{10,11... | collective-permute-start | bytes 7077896 | tf_op jit(solution)/shard_map/ppermute | solution.py:620
  1.2 26.4 %collective-permute-start.1 = (bf16[1536,768]{1,0:T(8,128)(2,1)}, bf16[1536,768]{1,0:T(8,128)(2,1)S(1)}, u32[]{:S(2)}, u32[]{:S(2)}) collective-permute-start(bf16[1536,768]{1,0:T(8,128)(2,1)} %down_a.3), channel_id=1, source_target_pairs={{0,1},{1,0},{2,3},{3,2},{4,5},{5,4},{6,7},{7,6},{8,9},{9,8},{10,11... | collective-permute-start | bytes 7077896 | tf_op jit(solution)/shard_map/ppermute | solution.py:621
  27.6 1.4 %copy-start = (bf16[768,1536]{1,0:T(8,128)(2,1)}, bf16[768,1536]{1,0:T(8,128)(2,1)S(1)}, u32[]{:S(2)}) copy-start(bf16[768,1536]{1,0:T(8,128)(2,1)S(1)} %collective-permute-done.up_b) | copy-start | bytes 7077892
  27.6 2.1 %copy-start.1 = (bf16[1536,768]{1,0:T(8,128)(2,1)}, bf16[1536,768]{1,0:T(8,128)(2,1)S(1)}, u32[]{:S(2)}) copy-start(bf16[1536,768]{1,0:T(8,128)(2,1)S(1)} %collective-permute-done.1.down_b) | copy-start | bytes 7077892

commit v4 on v3

--- a/solution.py
+++ b/solution.py
@@ -20,7 +20,7 @@
 ANY = pl.BlockSpec(memory_space=pl.ANY)
 VM = pl.BlockSpec(memory_space=pltpu.VMEM)
 SM = pl.BlockSpec(memory_space=pltpu.SMEM)
-LIMIT = 56 * 1024 * 1024
+LIMIT = 62 * 1024 * 1024
 
 
 def normed(values):
@@ -511,7 +511,7 @@
     rows_own, width = h.shape
     units = up_a.shape[1]
     return pl.pallas_call(
-        functools.partial(mlp_kernel, 256, 512),
+        functools.partial(mlp_kernel, 512, 512),
         out_shape=jax.ShapeDtypeStruct((final_t.shape[0], rows_own), BF16),
         in_specs=[VM] * 5 + [ANY] * 4,
         out_specs=VM,

time: 102 us -> 98.1 us (0.962)
  Pallas kernels: 95.2 us -> 93 us
  local copies, waits for them, and re-layouts: 4.7 us -> 2.65 us
    pallas_call x2, Pallas kernels: 24.2 us -> 21.8 us  [run_mlp(): pl.pallas_call(functools.partial(mlp_kernel, 512, 512), out_shape=jax.Sha...]
    unnamed x6 -> x2, local copies, waits for them, and re-layouts: 4.7 us -> 2.65 us
  transfers between devices with their start and end apart: 2 -> 2, of which waited for: 0 -> 0; matrix products, arithmetic and copies ran while one was open for 0% -> 0% of each run, Pallas kernels for 25% -> 26%
where the time goes in v4:
time: 98.1 us; the launch traced here: 97.6 us
  Pallas kernels  93 us (95%)
  local copies, waits for them, and re-layouts  2.65 us (3%)
  between operations  1.36 us (1%)
    pallas_call x2, Pallas kernels, run_attention(): pl.pallas_call(functools.partial(attention_kernel, tile), out_shape=jax.S...  39.5 us
    pallas_call x2, Pallas kernels, run_prefix(): pl.pallas_call(functools.partial(prefix_kernel, count, inner, last), out_...  25.6 us
    pallas_call x2, Pallas kernels, run_mlp(): pl.pallas_call(functools.partial(mlp_kernel, 512, 512), out_shape=jax.Sha...  21.8 us
    pallas_call x1, Pallas kernels, run_setup(): pl.pallas_call(setup_kernel, out_shape=(jax.ShapeDtypeStruct((8, width),...  6.12 us
    unnamed x2, local copies, waits for them, and re-layouts  2.65 us
  transfers between devices with their start and end apart: 2, of which 0 were waited for; matrix products, arithmetic and copies ran while one was open for 0% of the time, Pallas kernels for 26%

profile of v4, /device:TPU:0, one launch (start us, length us, event | category | flops | bytes accessed | tf_op | source)
XLA Modules:
  0.0 97.6 jit_solution(9377412824929882799)
XLA Ops:
  0.6 0.6 collective-permute-start
  1.2 0.1 collective-permute-start.1
  1.9 6.1 %setup.1 = (f32[8,768]{1,0:T(8,128)}, f32[8,128]{1,0:T(8,128)}, f32[8,128]{1,0:T(8,128)}, f32[2,16,512]{2,1,0:T(8,128)}, f32[16,1024]{1,0:T(8,128)}) custom-call(s32[17]{0:T(128)} %times_ref.1, s32[1,1]{1,0:T(1,128)S(6)} %copy.24.label_ref, f32[128,128]{1,0:T(8,128)} %bitcast.5, f32[1,2]{1,0:T(1,128)} %bitcast.7, bf16[1000,768]{1,0:T(8,128)(2,1)} %table_hbm.1, ...), custom_call_target="tpu_custom_call" | custom-call | bytes 12000000 | tf_op jit(solution)/shard_map/setup/pallas_call | solution.py:572
  8.1 19.7 %attention.2.h_ref = f32[512,768]{1,0:T(8,128)} custom-call(f32[16,1024]{1,0:T(8,128)} %get-tuple-element.13.x_ref, bf16[16,768]{1,0:T(8,128)(2,1)} %patch_ref.3, f32[128,384]{1,0:T(8,128)} %constant.8.clone.far_sin, f32[128,384]{1,0:T(8,128)} %constant.9.clone.far_cos, f32[8,384]{1,0:T(8,128)} %constant.10.clone.near_sin, ...), custom_call_target="tpu_custom_call" | custom-call | flops 10066329600 | bytes 8000000 | tf_op jit(solution)/shard_map/attention/pallas_call | solution.py:486
  27.8 0.0 collective-permute-done.up_b
  27.8 0.0 collective-permute-done.1.down_b
  27.8 10.9 %feed_forward.2.d_ref = bf16[16,512]{1,0:T(8,128)(2,1)} custom-call(f32[8,128]{1,0:T(8,128)} %get-tuple-element.12.coef_ref, f32[16,1024]{1,0:T(8,128)} %get-tuple-element.13.x_ref, f32[512,768]{1,0:T(8,128)} %attention.2.h_ref, f32[8,768]{1,0:T(8,128)} %get-tuple-element.14.mod_ref, bf16[16,768]{1,0:T(8,128)(2,1)} %bitcast.8, bf16[768,1536]{1,0:T(8,128)(2,1)} %up_a.3, ...), custom_call_target="tpu_custom_call" | custom-call | flops 4831838208 | bytes 12000000 | tf_op jit(solution)/shard_map/feed_forward/pallas_call | solution.py:513
  38.7 13.8 %prefix.1 = (f32[2,16,512]{2,1,0:T(8,128)}, f32[16,1024]{1,0:T(8,128)}, f32[8,128]{1,0:T(8,128)}) custom-call(bf16[16,512]{1,0:T(8,128)(2,1)} %feed_forward.2.d_ref, f32[2,16,512]{2,1,0:T(8,128)} %get-tuple-element.15.noise_ref, f32[8,128]{1,0:T(8,128)} %get-tuple-element.16.mix_ref), custom_call_target="tpu_custom_call" | custom-call | tf_op jit(solution)/shard_map/prefix/pallas_call | solution.py:544
  52.4 19.8 %attention.3.h_ref = f32[512,768]{1,0:T(8,128)} custom-call(f32[16,1024]{1,0:T(8,128)} %get-tuple-element.17.x_ref, bf16[16,768]{1,0:T(8,128)(2,1)} %patch_ref.3, f32[128,384]{1,0:T(8,128)} %constant.8.clone.far_sin, f32[128,384]{1,0:T(8,128)} %constant.9.clone.far_cos, f32[8,384]{1,0:T(8,128)} %constant.10.clone.near_sin, ...), custom_call_target="tpu_custom_call" | custom-call | flops 10066329600 | bytes 8000000 | tf_op jit(solution)/shard_map/attention/pallas_call | solution.py:486
  72.2 10.9 %feed_forward.3.d_ref = bf16[16,512]{1,0:T(8,128)(2,1)} custom-call(f32[8,128]{1,0:T(8,128)} %get-tuple-element.12.coef_ref, f32[16,1024]{1,0:T(8,128)} %get-tuple-element.17.x_ref, f32[512,768]{1,0:T(8,128)} %attention.3.h_ref, f32[8,768]{1,0:T(8,128)} %get-tuple-element.14.mod_ref, bf16[16,768]{1,0:T(8,128)(2,1)} %bitcast.9, bf16[768,1536]{1,0:T(8,128)(2,1)} %up_a.3, ...), custom_call_target="tpu_custom_call" | custom-call | flops 4831838208 | bytes 12000000 | tf_op jit(solution)/shard_map/feed_forward/pallas_call | solution.py:513
  83.1 11.9 %prefix_last.1 = (f32[128,128]{1,0:T(8,128)}, f32[1,2]{1,0:T(1,128)}) custom-call(bf16[16,512]{1,0:T(8,128)(2,1)} %feed_forward.3.d_ref, f32[2,16,512]{2,1,0:T(8,128)} %get-tuple-element.15.noise_ref, f32[8,128]{1,0:T(8,128)} %get-tuple-element.16.mix_ref, f32[2,16,512]{2,1,0:T(8,128)} %get-tuple-element.18.rest_0_, f32[8,128]{1,0:T(8,128)} %get-tuple-element.19.rest_1_), custom_call_target="tpu_custom_call" | custom-call | tf_op jit(solution)/shard_map/prefix_last/pallas_call | solution.py:544
  95.0 1.5 %copy.25 = f32[1,1,16384]{2,1,0:T(1,128)} copy(f32[1,1,16384]{2,1,0:T(1,128)} %bitcast.6) | data formatting | bytes 131072
  96.5 1.2 %copy.26 = f32[2,1]{0,1:T(1,128)} copy(f32[2,1]{0,1:T(1,128)} %bitcast.10) | data formatting | bytes 16
Async XLA Ops:
  0.6 27.1 %collective-permute-start = (bf16[768,1536]{1,0:T(8,128)(2,1)}, bf16[768,1536]{1,0:T(8,128)(2,1)}, u32[]{:S(2)}, u32[]{:S(2)}) collective-permute-start(bf16[768,1536]{1,0:T(8,128)(2,1)} %up_a.3), channel_id=1, source_target_pairs={{0,1},{1,0},{2,3},{3,2},{4,5},{5,4},{6,7},{7,6},{8,9},{9,8},{10,11... | collective-permute-start | bytes 7077896 | tf_op jit(solution)/shard_map/ppermute | solution.py:620
  1.2 26.6 %collective-permute-start.1 = (bf16[1536,768]{1,0:T(8,128)(2,1)}, bf16[1536,768]{1,0:T(8,128)(2,1)}, u32[]{:S(2)}, u32[]{:S(2)}) collective-permute-start(bf16[1536,768]{1,0:T(8,128)(2,1)} %down_a.3), channel_id=1, source_target_pairs={{0,1},{1,0},{2,3},{3,2},{4,5},{5,4},{6,7},{7,6},{8,9},{9,8},{10,11... | collective-permute-start | bytes 7077896 | tf_op jit(solution)/shard_map/ppermute | solution.py:621
